TPU v7x, 32 devices: a whole 2x2x4 slice. The times are simulated.
32 devices in a mesh: cols: 4 (over y, core), levs: 2 (over x), owner: 4 (over z).
Axes of the slice: x: 2, y: 2, z: 4, core: 2. Of those that a mesh axis runs over, the one named last changes fastest.
Arguments:
- perturbations: bfloat16 [80, 32, 4096], P(None, 'levs', 'cols'), may hold values from -8 to 8
- background: float32 [32, 4096], P('levs', 'cols'), may hold values from -6 to 6
- obs_cols: int32 [4, 2048], P(None, 'owner'), may hold values from 0 to 4095, as said below
- obs_levs: int32 [4, 2048], P(None, 'owner'), may hold values from 0 to 31
- obs_vals: float32 [4, 2048], P(None, 'owner'), may hold values from -12 to 12
- obs_sigma: float32 [4, 2048], P(None, 'owner'), may hold values from 2 to 4
- pairs: int32 [4, 32, 16], P(None, 'cols'), may hold values 0 or 1
Outputs:
- analysis_mean: float32 [32, 4096], P('levs', 'cols')
- analysis_pert: bfloat16 [80, 32, 4096], P(None, 'levs', 'cols')
Inputs may be any that keep to these rules, and one draw needn't show every extreme that they name: `obs_cols`: for each batch, the 512 observations held by one owner index fall in the columns of one cols index (a run of 1024 columns) at most 384 times, and exactly 384 times for some cols index.
All inputs are finite; a program needn't handle non-finite values. No bound on the sum of `pairs` on one device may be relied on, other than what follows from the above.
Results may differ from a plain program's by a relative error of at most 0.0088.
Values sent between devices are 32-bit elements; how exact they have to be, the bound alone decides.
No kernel may reach another device: no remote copies, remote signals or barrier semaphores. Data moves between devices by JAX's collectives and lax.ppermute only.
A program may use at most 64 MiB of HBM per device.

v0:
```python
import functools
import math

import jax
import jax.numpy as jnp
from jax import lax
from jax.experimental import pallas as pl
from jax.experimental.pallas import tpu as pltpu
from jax.sharding import PartitionSpec as P

F32 = jnp.float32
BF16 = jnp.bfloat16
LANES = 128
GROUP = 8
CHUNK = 32
PACK = LANES // CHUNK
DROWS = 96
VMEM_BYTES = 40 << 20


def params():
    return pltpu.CompilerParams(vmem_limit_bytes=VMEM_BYTES)


def split2(x):
    high = x.astype(BF16)
    return high, (x - high.astype(F32)).astype(BF16)


def nt_dot(a, b):
    return lax.dot_general(a, b, (((1,), (1,)), ((), ())), preferred_element_type=F32)


def observe_into(y_ref, hot_ref, pert_ref, mean_ref, local_cols, local_levs):
    col_dev, count = hot_ref.shape
    lev_dev = mean_ref.shape[0]
    members = pert_ref.shape[0] // lev_dev
    for start in range(0, col_dev, 256):
        rows = lax.broadcasted_iota(jnp.int32, (256, count), 0) + start
        hot_ref[start : start + 256, :] = jnp.where(rows == local_cols, 1.0, 0.0).astype(BF16)
    lev_hot = lax.broadcasted_iota(jnp.int32, (lev_dev, count), 0) == local_levs
    hot = hot_ref[...]
    step = 16
    for start in range(0, members, step):
        picked = jnp.dot(
            pert_ref[start * lev_dev : (start + step) * lev_dev, :], hot, preferred_element_type=F32
        ).reshape(step, lev_dev, count)
        y_ref[start : start + step, :] = jnp.sum(jnp.where(lev_hot[None], picked, 0.0), axis=1)
    mean = mean_ref[...]
    high = mean.astype(BF16)
    rest = mean - high.astype(F32)
    middle = rest.astype(BF16)
    low = (rest - middle.astype(F32)).astype(BF16)
    picked = jnp.dot(jnp.concatenate([high, middle, low], axis=0), hot, preferred_element_type=F32)
    picked = (
        picked[:lev_dev] + picked[lev_dev : 2 * lev_dev] + picked[2 * lev_dev : 3 * lev_dev]
    )
    total = jnp.sum(jnp.where(lev_hot, picked, 0.0), axis=0, keepdims=True)
    tail = y_ref.shape[0] - members
    first = lax.broadcasted_iota(jnp.int32, (tail, count), 0) == 0
    y_ref[members:, :] = jnp.where(first, jnp.broadcast_to(total, (tail, count)), 0.0)


def block_grams(values, mean_row, sigma, vals, members, store):
    root = math.sqrt(members - 1.0)
    count = values.shape[1]
    scale = 1.0 / (sigma * root)
    innov = (vals - mean_row) / sigma
    wide = values.astype(F32) * (scale * scale)
    pad = LANES - members
    first = lax.broadcasted_iota(jnp.int32, (pad, count), 0) == 0
    last = jnp.where(first, jnp.broadcast_to(scale * innov, (pad, count)), 0.0)
    high, low = split2(jnp.concatenate([wide, last], axis=0))
    for block in range(count // LANES):
        at = slice(block * LANES, (block + 1) * LANES)
        left = jnp.concatenate([values[:, at], values[:, at]], axis=1)
        right = jnp.concatenate([high[:, at], low[:, at]], axis=1)
        store(block, nt_dot(left, right))


def first_kernel(pert_ref, mean_ref, cols_ref, levs_ref, sigma_ref, vals_ref, keep_ref, send_ref, y_ref, hot_ref):
    observe_into(y_ref, hot_ref, pert_ref, mean_ref, cols_ref[...], levs_ref[...])
    members = keep_ref.shape[1]
    own_blocks = keep_ref.shape[0]

    def store(block, product):
        if block < own_blocks:
            keep_ref[block] = product
        else:
            send_ref[block - own_blocks] = product

    block_grams(
        y_ref[:members, :].astype(BF16), y_ref[members : members + 1, :], sigma_ref[...], vals_ref[...], members, store
    )


def observe_kernel(pert_ref, mean_ref, cols_ref, levs_ref, keep_ref, send_ref, y_ref, hot_ref):
    observe_into(y_ref, hot_ref, pert_ref, mean_ref, cols_ref[0], levs_ref[0])
    half = keep_ref.shape[2]
    keep_ref[0] = y_ref[:, :half]
    send_ref[0] = y_ref[:, half:]


def tile_lanes(shape):
    return lax.broadcasted_iota(jnp.int32, shape, 1)


def build_systems(s_ref, pairs, order_ref, own_ref, peer_ref):
    members = own_ref.shape[1]
    spread = nt_dot(order_ref[...], jnp.concatenate([pairs.astype(BF16)] * GROUP, axis=0))
    row = lax.broadcasted_iota(jnp.int32, spread.shape, 0)
    lane = tile_lanes(spread.shape)
    select = jnp.where(row % GROUP == lane // CHUNK, spread, 0.0).astype(BF16)
    rows = s_ref.shape[1]
    out_row = lax.broadcasted_iota(jnp.int32, (rows, LANES), 0)
    out_pack = tile_lanes((rows, LANES)) // CHUNK
    for start in range(0, members, GROUP):
        at = slice(start, start + GROUP)
        stacked = jnp.concatenate(
            [ref[block, at, :] for ref in (own_ref, peer_ref) for block in range(ref.shape[0])], axis=0
        )
        high, low = split2(stacked.T[:rows])
        product = jnp.dot(jnp.concatenate([high, low], axis=1), select, preferred_element_type=F32)
        for part in range(GROUP // PACK):
            first = start + part * PACK
            s_ref[first // PACK] = product[:, part * LANES : (part + 1) * LANES] + jnp.where(
                out_row == first + out_pack, 1.0, 0.0
            )


def invert_factors(s_ref, r_ref, w_ref, members):
    rows = s_ref.shape[1]
    pack = tile_lanes((rows, LANES)) // CHUNK
    within = tile_lanes((rows, LANES)) % CHUNK
    group_row = lax.broadcasted_iota(jnp.int32, (GROUP, LANES), 0)
    count = members // GROUP
    weights = [jnp.zeros((GROUP, LANES), F32) for _ in range(count)]
    picks = [within + p * CHUNK for p in range(PACK)]
    for s in range(count):
        start = s * GROUP
        first = start // PACK
        copies = []
        for a in range(GROUP):
            copies.append(jnp.take_along_axis(s_ref[first + a // PACK], picks[a % PACK], axis=1))
        entry = [[None] * GROUP for _ in range(GROUP)]
        for a in range(GROUP):
            for b in range(a, GROUP):
                entry[a][b] = jnp.broadcast_to(copies[a][start + b : start + b + 1, :], (GROUP, LANES))
        ratio = [[None] * GROUP for _ in range(GROUP)]
        inverse = [None] * GROUP
        for a in range(GROUP):
            inverse[a] = 1.0 / entry[a][a]
            for b in range(a + 1, GROUP):
                ratio[b][a] = entry[a][b] * inverse[a]
            for b in range(a + 1, GROUP):
                for c in range(b, GROUP):
                    entry[b][c] = entry[b][c] - ratio[b][a] * entry[a][c]
        roots = [lax.rsqrt(entry[a][a]) for a in range(GROUP)]
        pieces = rows // GROUP
        lower = [[None] * pieces for _ in range(GROUP)]
        for v in range(pieces):
            for a in range(GROUP):
                if v == s:
                    value = jnp.where(group_row == a, 1.0, 0.0)
                else:
                    value = copies[a][v * GROUP : (v + 1) * GROUP, :]
                for b in range(a):
                    value = value - ratio[a][b] * lower[b][v]
                lower[a][v] = value
        more = start + GROUP < members
        if more:
            for v in range(pieces):
                solved = [None] * GROUP
                for a in range(GROUP - 1, -1, -1):
                    value = lower[a][v] * inverse[a]
                    for b in range(a + 1, GROUP):
                        value = value - ratio[b][a] * solved[b]
                    solved[a] = value
                for a in range(GROUP):
                    value = solved[a]
                    if v == s:
                        value = value + jnp.where(group_row == a, 1.0, 0.0)
                    r_ref[a, v * GROUP : (v + 1) * GROUP, :] = value
        for part in range(GROUP // PACK):

            def merged(v):
                value = lower[part * PACK][v] * roots[part * PACK]
                for p in range(1, PACK):
                    a = part * PACK + p
                    value = jnp.where(pack[:GROUP] == p, lower[a][v] * roots[a], value)
                return value

            halfway = jnp.broadcast_to(merged(count)[0:1, :], (GROUP, LANES))
            for v in range(count):
                if v <= s:
                    value = merged(v)
                    weights[v] = weights[v] + halfway * value
                else:
                    value = jnp.zeros((GROUP, LANES), F32)
                s_ref[first + part, v * GROUP : (v + 1) * GROUP, :] = value
        if more:

            def trailing(index, carry, s=s, start=start, first=first):
                for step in range(GROUP // PACK):
                    block = first + (index + 1) * (GROUP // PACK) + step
                    old = s_ref[block, start : start + GROUP, :]
                    factors = [jnp.broadcast_to(old[a : a + 1, :], (GROUP, LANES)) for a in range(GROUP)]
                    for v in range(pieces):
                        at = slice(v * GROUP, (v + 1) * GROUP)
                        value = s_ref[block, at, :]
                        for a in range(GROUP):
                            value = value - factors[a] * r_ref[a, at, :]
                        s_ref[block, at, :] = value
                return carry

            lax.fori_loop(0, count - 1 - s, trailing, 0)
    for v in range(count):
        total = weights[v]
        shift = CHUNK
        while shift < LANES:
            total = total + pltpu.roll(total, shift, 1)
            shift *= 2
        w_ref[v * GROUP : (v + 1) * GROUP, :] = total


def by_tile(s_ref, w_ref, m_ref, wrow_ref, members):
    one = jnp.where(
        lax.broadcasted_iota(jnp.int32, (LANES, LANES), 0) == tile_lanes((LANES, LANES)), 1.0, 0.0
    ).astype(BF16)
    pad = jnp.zeros((LANES - members, LANES), BF16)
    for block in range(members // PACK):
        value = jnp.concatenate([s_ref[block, :members, :].astype(BF16), pad], axis=0)
        m_ref[block * LANES : (block + 1) * LANES, :] = nt_dot(one, value)
    value = jnp.concatenate([w_ref[...].astype(BF16), pad], axis=0)
    wrow_ref[...] = nt_dot(one[:CHUNK], value)


def factor_chunk(pairs, order_ref, own_ref, peer_ref, s_ref, r_ref, w_ref, m_ref, wrow_ref):
    members = own_ref.shape[1]
    build_systems(s_ref, pairs, order_ref, own_ref, peer_ref)
    invert_factors(s_ref, r_ref, w_ref, members)
    by_tile(s_ref, w_ref, m_ref, wrow_ref, members)


def factor_scratch(members):
    return [
        pltpu.VMEM((members // PACK, members + GROUP, LANES), F32),
        pltpu.VMEM((GROUP, members + GROUP, LANES), F32),
        pltpu.VMEM((members, LANES), F32),
        pltpu.VMEM((members * CHUNK, LANES), F32),
        pltpu.VMEM((CHUNK, LANES), F32),
    ]


def product_of(m_ref, w_ref, tile, old, members):
    rows = m_ref[pl.ds(tile, members, stride=CHUNK), :].astype(BF16)
    tail = DROWS - members
    sub = lax.broadcasted_iota(jnp.int32, (tail, LANES), 0)
    lane = lax.broadcasted_iota(jnp.int32, (tail, LANES), 1)
    weights = jnp.broadcast_to(w_ref[pl.ds(tile, 1), :], (tail, LANES))
    if old is None:
        return jnp.concatenate([rows, jnp.where(sub == 0, weights, 0.0).astype(BF16)], axis=0), None
    ones = (lane >= members) & (lane < members + 2)
    extra = jnp.where(sub == 0, jnp.where(ones, 1.0, weights), 0.0).astype(BF16)
    left = jnp.concatenate([rows, extra], axis=0)[:, :DROWS]
    new = jnp.dot(left, old[0], preferred_element_type=F32)
    if old[1] is not None:
        new = new + jnp.dot(left, old[1], preferred_element_type=F32)
    total = jnp.broadcast_to(new[members : members + 1, :], (tail, LANES))
    high = total.astype(BF16).astype(F32)
    last = jnp.where(sub == 0, high, jnp.where(sub == 1, total - high, 0.0))
    return split2(jnp.concatenate([new[:members], last], axis=0))


def products(m_ref, w_ref, old_ref, new_ref, base, pairs_of, members):
    def pair(index, carry):
        for side in range(2):
            at = slice(side * LANES, (side + 1) * LANES)
            low_at = slice((side + 2) * LANES, (side + 3) * LANES)
            old = None
            if old_ref is not None:
                old = old_ref[base + index, :, at], None
                if old_ref.shape[2] > 2 * LANES:
                    old = old[0], old_ref[base + index, :, low_at]
            high, low = product_of(m_ref, w_ref, index * 2 + side, old, members)
            new_ref[base + index, :, at] = high
            if low is not None:
                new_ref[base + index, :, low_at] = low
        return carry

    lax.fori_loop(0, pairs_of, pair, 0, unroll=2)


def batch_kernel(first, *refs):
    if first:
        (pair_ref, order_ref, own_ref, peer_ref, y_ref, tile_ref, sigma_ref, vals_ref, new_ref, gram_ref, x_ref, *factor) = refs
        old_ref = None
    else:
        (pair_ref, order_ref, own_ref, peer_ref, y_ref, tile_ref, sigma_ref, vals_ref, old_ref, new_ref, gram_ref, x_ref, *factor) = refs
    members = own_ref.shape[1]
    root = math.sqrt(members - 1.0)
    chunks = pair_ref.shape[0] // CHUNK

    def one_chunk(index):
        pairs = pair_ref[pl.ds(index * CHUNK, CHUNK), :]
        factor_chunk(pairs, order_ref, own_ref, peer_ref, *factor)
        products(factor[3], factor[4], old_ref, new_ref, index * (CHUNK // 2), CHUNK // 2, members)

    if chunks == 1:
        one_chunk(0)
    else:
        pl.loop(0, chunks)(one_chunk)
    tile = tile_ref[...]
    count = tile.shape[1]
    start_values = y_ref[:members, :]
    empty = jnp.zeros((LANES - members, count), BF16)
    for side in range(2):
        x_ref[side * LANES : side * LANES + members, :] = jnp.where(tile % 2 == side, start_values, 0.0).astype(BF16)
        x_ref[side * LANES + members : (side + 1) * LANES, :] = empty
    parts = new_ref.shape[2] // (2 * LANES)
    stacked = jnp.concatenate([x_ref[...]] * parts, axis=0)
    half_tile = tile // 2
    per = 4

    def gather(index, total):
        at = new_ref[pl.ds(index * per, per)].reshape(per * DROWS, new_ref.shape[2])
        product = jnp.dot(at, stacked, preferred_element_type=F32)
        for k in range(per):
            total = jnp.where(half_tile == index * per + k, product[k * DROWS : (k + 1) * DROWS], total)
        return total

    now = lax.fori_loop(0, new_ref.shape[0] // per, gather, jnp.zeros((DROWS, count), F32))
    mean_row = y_ref[members : members + 1, :] + (now[members : members + 1] + now[members + 1 : members + 2]) / root

    def store(block, product):
        gram_ref[block] = product

    block_grams(now[:members].astype(BF16), mean_row, sigma_ref[...], vals_ref[...], members, store)


def last_kernel(pair_ref, order_ref, own_ref, peer_ref, old_ref, pert_ref, mean_ref, out_mean_ref, out_ref, new_ref, *factor):
    members = own_ref.shape[1]
    root = math.sqrt(members - 1.0)
    factor_chunk(pair_ref[...], order_ref, own_ref, peer_ref, *factor)
    products(factor[3], factor[4], old_ref, new_ref, 0, new_ref.shape[0], members)
    tiles = new_ref.shape[0] * 2
    width = pert_ref.shape[2] // tiles
    for tile in range(tiles):
        side = tile % 2
        left = new_ref[tile // 2, :, side * LANES : side * LANES + members]
        left_low = new_ref[tile // 2, :, (side + 2) * LANES : (side + 2) * LANES + members]
        at = slice(tile * width, (tile + 1) * width)
        for lev in range(pert_ref.shape[0]):
            pert = pert_ref[lev, :, at]
            new = jnp.dot(left, pert, preferred_element_type=F32) + jnp.dot(
                left_low, pert, preferred_element_type=F32
            )
            out_ref[lev, :, at] = new[:members].astype(BF16)
            gain = new[members : members + 1] + new[members + 1 : members + 2]
            out_mean_ref[lev : lev + 1, at] = mean_ref[lev : lev + 1, at] + gain / root


def swap(x, axis, bit):
    return lax.ppermute(x, axis, [(i, i ^ bit) for i in range(lax.axis_size(axis))])


def upper_bits(axis, first):
    bit, bits = first, []
    while bit < lax.axis_size(axis):
        bits.append(bit)
        bit *= 2
    return bits


def plane_sum(keep, send):
    total = keep + swap(send, "cols", 1)
    for bit in upper_bits("cols", 2):
        total = total + swap(total, "cols", bit)
    for bit in upper_bits("levs", 1):
        total = total + swap(total, "levs", bit)
    return total


def body(perturbations, background, obs_cols, obs_levs, obs_vals, obs_sigma, pairs):
    members, lev_dev, col_dev = perturbations.shape
    batches, obs_own = obs_cols.shape
    tiles_dev, block_count = pairs.shape[1:]
    tile_cols = col_dev // tiles_dev
    cols_size, owners = lax.axis_size("cols"), lax.axis_size("owner")
    tiles = tiles_dev * cols_size
    own_blocks = block_count // owners // 2
    half = obs_own // 2
    cols_index = lax.axis_index("cols")
    core = cols_index % 2
    owner = lax.axis_index("owner")

    def halves(x):
        parts = x.reshape(batches, 2, half)
        return jnp.where(core == 0, parts, parts[:, ::-1])

    cols_half = halves(obs_cols)
    local_cols = (cols_half - cols_index * col_dev).reshape(batches, 1, obs_own)
    local_levs = (halves(obs_levs) - lax.axis_index("levs") * lev_dev).reshape(batches, 1, obs_own)
    sigma_half = halves(obs_sigma)
    vals_half = halves(obs_vals)
    tile_half = cols_half[:, 0] // tile_cols

    all_pairs = pairs.astype(F32)
    for bit in upper_bits("cols", 1):
        other = swap(all_pairs, "cols", bit)
        upper = (cols_index // bit) % 2 == 1
        all_pairs = jnp.where(
            upper, jnp.concatenate([other, all_pairs], axis=1), jnp.concatenate([all_pairs, other], axis=1)
        )

    place = jnp.arange(2 * block_count * GROUP) // GROUP % block_count
    side, rest = place // (block_count // 2), place % (block_count // 2)
    hop, block = rest // own_blocks, rest % own_blocks
    wanted = (owner ^ hop) * (2 * own_blocks) + (core ^ side) * own_blocks + block
    order = (wanted[:, None] == jnp.arange(block_count)[None, :]).astype(BF16)

    flat = perturbations.reshape(members * lev_dev, col_dev)
    gram = jax.ShapeDtypeStruct((own_blocks, members, LANES), F32)
    observed_scratch = [pltpu.VMEM((88, obs_own), F32), pltpu.VMEM((col_dev, obs_own), BF16)]
    keep, send = pl.pallas_call(
        first_kernel,
        out_shape=(gram, gram),
        scratch_shapes=observed_scratch,
        compiler_params=params(),
        name="first",
    )(
        flat,
        background,
        local_cols[0],
        local_levs[0],
        sigma_half[0].reshape(1, obs_own),
        vals_half[0].reshape(1, obs_own),
    )
    later = jax.ShapeDtypeStruct((batches - 1, 88, half), F32)
    row_spec = pl.BlockSpec((1, 1, obs_own), lambda k: (k, 0, 0))
    out_spec = pl.BlockSpec((1, 88, half), lambda k: (k, 0, 0))
    y_keep, y_send = pl.pallas_call(
        observe_kernel,
        grid=(batches - 1,),
        in_specs=[
            pl.BlockSpec(flat.shape, lambda k: (0, 0)),
            pl.BlockSpec(background.shape, lambda k: (0, 0)),
            row_spec,
            row_spec,
        ],
        out_specs=(out_spec, out_spec),
        out_shape=(later, later),
        scratch_shapes=observed_scratch,
        compiler_params=params(),
        name="observe",
    )(flat, background, local_cols[1:], local_levs[1:])

    gram_own = plane_sum(keep, send)
    observed = plane_sum(y_keep, y_send)
    by_level = jnp.transpose(perturbations, (1, 0, 2))

    def spread(gram_own):
        own = jnp.concatenate([gram_own] + [swap(gram_own, "owner", hop) for hop in range(1, owners)], axis=0)
        return own, swap(own, "cols", 1)

    product = None
    for index in range(batches - 1):
        own, peer = spread(gram_own)
        operands = [
            all_pairs[index],
            order,
            own,
            peer,
            observed[index],
            tile_half[index + 1].reshape(1, half),
            sigma_half[index + 1, 0].reshape(1, half),
            vals_half[index + 1, 0].reshape(1, half),
        ]
        if index:
            operands.append(product)
        product, gram_own = pl.pallas_call(
            functools.partial(batch_kernel, index == 0),
            out_shape=(jax.ShapeDtypeStruct((tiles // 2, DROWS, (4 if index else 2) * LANES), BF16), gram),
            scratch_shapes=[
                pltpu.VMEM((2 * LANES, half), BF16),
                *factor_scratch(members),
            ],
            compiler_params=params(),
            name="batch",
        )(*operands)

    own, peer = spread(gram_own)
    pairs_of = tiles_dev // 2
    own_product = lax.dynamic_slice_in_dim(product, cols_index * pairs_of, pairs_of, 0)
    mean, out = pl.pallas_call(
        last_kernel,
        out_shape=(
            jax.ShapeDtypeStruct(background.shape, F32),
            jax.ShapeDtypeStruct(by_level.shape, BF16),
        ),
        scratch_shapes=[
            pltpu.VMEM((pairs_of, DROWS, 4 * LANES), BF16),
            *factor_scratch(members),
        ],
        compiler_params=params(),
        name="last",
    )(
        jnp.pad(pairs[batches - 1].astype(F32), ((0, CHUNK - tiles_dev), (0, 0))),
        order, own, peer, own_product, by_level, background)
    return mean, jnp.transpose(out, (1, 0, 2))


def solution(mesh):
    return jax.shard_map(
        body,
        mesh=mesh,
        in_specs=(
            P(None, "levs", "cols"),
            P("levs", "cols"),
            P(None, "owner"),
            P(None, "owner"),
            P(None, "owner"),
            P(None, "owner"),
            P(None, "cols", None),
        ),
        out_specs=(P("levs", "cols"), P(None, "levs", "cols")),
        check_vma=False,
    )
```

profile of v0, /device:TPU:0, one launch (start us, length us, event | category | flops | bytes accessed | tf_op | source)
XLA Modules:
  0.0 118.3 jit_solution(3049382975429478258)
XLA Ops:
  4.2 1.7 %copy-done = bf16[80,16,1024]{2,1,0:T(8,128)(2,1)S(1)} copy-done((bf16[80,16,1024]{2,1,0:T(8,128)(2,1)S(1)}, bf16[80,16,1024]{2,1,0:T(8,128)(2,1)}, u32[]{:S(2)}) %copy-start) | copy-done | bytes 2621464
  6.8 2.1 %first.1 = (f32[2,80,128]{2,1,0:T(8,128)S(1)}, f32[2,80,128]{2,1,0:T(8,128)S(1)}) custom-call(bf16[1280,1024]{1,0:T(8,128)(2,1)S(1)} %bitcast.45, f32[16,1024]{1,0:T(8,128)S(1)} %copy-done.5, s32[1,512]{1,0:T(1,128)S(1)} %bitcast.50, s32[1,512]{1,0:T(1,128)S(1)} %bitcast.49, f32[1,512]{1,0:T(1,128)S(1)} %bitcast.52, f32[1,512]{1,0:T(1,128)S(1)} %bitcast.51), custom_call_target="tpu_custom_call" | custom-call | tf_op jit(solution)/shard_map/first/pallas_call | solution.py:425
  9.0 5.7 %observe.1 = (f32[3,88,256]{2,1,0:T(8,128)S(1)}, f32[3,88,256]{2,1,0:T(8,128)S(1)}) custom-call(bf16[1280,1024]{1,0:T(8,128)(2,1)S(1)} %bitcast.46, f32[16,1024]{1,0:T(8,128)S(1)} %copy-done.5, s32[3,1,512]{2,1,0:T(1,128)S(1)} %copy.11.cols_ref, s32[3,1,512]{2,1,0:T(1,128)S(1)} %copy.12.levs_ref), custom_call_target="tpu_custom_call" | custom-call | tf_op jit(solution)/shard_map/observe/pallas_call | solution.py:442
  15.5 2.6 %collective-permute-start.3 = (f32[2,80,128]{2,1,0:T(8,128)S(1)}, f32[2,80,128]{2,1,0:T(8,128)S(1)}, u32[]{:S(2)}, u32[]{:S(2)}) collective-permute-start(f32[2,80,128]{2,1,0:T(8,128)S(1)} %add.102), channel_id=1, source_target_pairs={{0,16},{8,24},{16,0},{24,8},{1,17},{9,25},{17,1},{25,9},{2,18},{10... | collective-permute-start | bytes 245768 | tf_op jit(solution)/shard_map/ppermute | solution.py:364
  18.2 3.2 %collective-permute-done.3 = f32[2,80,128]{2,1,0:T(8,128)S(1)} collective-permute-done((f32[2,80,128]{2,1,0:T(8,128)S(1)}, f32[2,80,128]{2,1,0:T(8,128)S(1)}, u32[]{:S(2)}, u32[]{:S(2)}) %collective-permute-start.3) | collective-permute-done | bytes 81952 | tf_op jit(solution)/shard_map/ppermute | solution.py:364
  21.4 1.9 %collective-permute-start.4 = (f32[2,80,128]{2,1,0:T(8,128)S(1)}, f32[2,80,128]{2,1,0:T(8,128)S(1)}, u32[]{:S(2)}, u32[]{:S(2)}) collective-permute-start(f32[2,80,128]{2,1,0:T(8,128)S(1)} %add.103), channel_id=1, source_target_pairs={{0,4},{4,0},{1,5},{5,1},{2,6},{6,2},{3,7},{7,3},{8,12},{12,8},{9,1... | collective-permute-start | bytes 245768 | tf_op jit(solution)/shard_map/ppermute | solution.py:364
  25.9 4.0 %collective-permute-start.7 = (f32[2,80,128]{2,1,0:T(8,128)S(1)}, f32[2,80,128]{2,1,0:T(8,128)S(1)}, u32[]{:S(2)}, u32[]{:S(2)}) collective-permute-start(f32[2,80,128]{2,1,0:T(8,128)S(1)} %add.104), channel_id=1, source_target_pairs={{0,3},{1,2},{2,1},{3,0},{4,7},{5,6},{6,5},{7,4},{8,11},{9,10},{10,... | collective-permute-start | bytes 245768 | tf_op jit(solution)/shard_map/ppermute | solution.py:364
  32.4 3.2 %collective-permute-done.6 = f32[2,80,128]{2,1,0:T(8,128)S(1)} collective-permute-done((f32[2,80,128]{2,1,0:T(8,128)S(1)}, f32[2,80,128]{2,1,0:T(8,128)S(1)}, u32[]{:S(2)}, u32[]{:S(2)}) %collective-permute-start.6) | collective-permute-done | bytes 81952 | tf_op jit(solution)/shard_map/ppermute | solution.py:364
  35.7 1.8 %collective-permute-done.11 = f32[3,88,256]{2,1,0:T(8,128)S(1)} collective-permute-done((f32[3,88,256]{2,1,0:T(8,128)S(1)}, f32[3,88,256]{2,1,0:T(8,128)S(1)}, u32[]{:S(2)}, u32[]{:S(2)}) %collective-permute-start.11) | collective-permute-done | bytes 270368 | tf_op jit(solution)/shard_map/ppermute | solution.py:364
  37.6 8.7 %batch.3 = (bf16[16,96,256]{2,1,0:T(8,128)(2,1)S(1)}, f32[2,80,128]{2,1,0:T(8,128)S(1)}) custom-call(f32[32,16]{1,0:T(8,128)S(1)} %get-tuple-element.35.refs_0_, bf16[256,16]{1,0:T(8,128)(2,1)S(1)} %fusion.refs_1_.order_ref, f32[8,80,128]{2,1,0:T(8,128)S(1)} %pad_maximum_fusion.refs_2_, f32[8,80,128]{2,1,0:T(8,128)S(1)} %collective-permute-done.8.refs_3_, ...), custom_call_target="tpu_custom_call" | custom-call | tf_op jit(solution)/shard_map/batch/pallas_call | solution.py:481
  46.3 3.7 %collective-permute-start.14 = (f32[2,80,128]{2,1,0:T(8,128)S(1)}, f32[2,80,128]{2,1,0:T(8,128)S(1)}, u32[]{:S(2)}, u32[]{:S(2)}) collective-permute-start(f32[2,80,128]{2,1,0:T(8,128)S(1)} %get-tuple-element.18), channel_id=1, source_target_pairs={{0,3},{1,2},{2,1},{3,0},{4,7},{5,6},{6,5},{7,4},{8,11},{9,10},{10,... | collective-permute-start | bytes 245768 | tf_op jit(solution)/shard_map/ppermute | solution.py:364
  50.7 3.9 %collective-permute-done.12 = f32[2,80,128]{2,1,0:T(8,128)S(1)} collective-permute-done((f32[2,80,128]{2,1,0:T(8,128)S(1)}, f32[2,80,128]{2,1,0:T(8,128)S(1)}, u32[]{:S(2)}, u32[]{:S(2)}) %collective-permute-start.12) | collective-permute-done | bytes 81952 | tf_op jit(solution)/shard_map/ppermute | solution.py:364
  54.7 2.1 %collective-permute-done.13 = f32[2,80,128]{2,1,0:T(8,128)S(1)} collective-permute-done((f32[2,80,128]{2,1,0:T(8,128)S(1)}, f32[2,80,128]{2,1,0:T(8,128)S(1)}, u32[]{:S(2)}, u32[]{:S(2)}) %collective-permute-start.13) | collective-permute-done | bytes 81952 | tf_op jit(solution)/shard_map/ppermute | solution.py:364
  58.5 9.8 %batch.4 = (bf16[16,96,512]{2,1,0:T(8,128)(2,1)S(1)}, f32[2,80,128]{2,1,0:T(8,128)S(1)}) custom-call(f32[32,16]{1,0:T(8,128)S(1)} %get-tuple-element.36.refs_0_, bf16[256,16]{1,0:T(8,128)(2,1)S(1)} %fusion.refs_1_.order_ref, f32[8,80,128]{2,1,0:T(8,128)S(1)} %constant_dynamic-update-slice_fusion.refs_2_, f32[8,80,128]{2,1,0:T(8,128)S(1)} %collective-permute-done.15.refs_3_, ...), custom_call_target="tpu_custom_call" | custom-call | tf_op jit(solution)/shard_map/batch/pallas_call | solution.py:481
  69.4 2.2 %collective-permute-start.18 = (f32[2,80,128]{2,1,0:T(8,128)S(1)}, f32[2,80,128]{2,1,0:T(8,128)S(1)}, u32[]{:S(2)}, u32[]{:S(2)}) collective-permute-start(f32[2,80,128]{2,1,0:T(8,128)S(1)} %get-tuple-element.20), channel_id=1, source_target_pairs={{0,3},{1,2},{2,1},{3,0},{4,7},{5,6},{6,5},{7,4},{8,11},{9,10},{10,... | collective-permute-start | bytes 245768 | tf_op jit(solution)/shard_map/ppermute | solution.py:364
  71.7 2.1 %collective-permute-start.16 = (f32[2,80,128]{2,1,0:T(8,128)S(1)}, f32[2,80,128]{2,1,0:T(8,128)S(1)}, u32[]{:S(2)}, u32[]{:S(2)}) collective-permute-start(f32[2,80,128]{2,1,0:T(8,128)S(1)} %get-tuple-element.20), channel_id=1, source_target_pairs={{0,1},{1,0},{2,3},{3,2},{4,5},{5,4},{6,7},{7,6},{8,9},{9,8},{10,11... | collective-permute-start | bytes 245768 | tf_op jit(solution)/shard_map/ppermute | solution.py:364
  73.8 4.5 %collective-permute-done.16 = f32[2,80,128]{2,1,0:T(8,128)S(1)} collective-permute-done((f32[2,80,128]{2,1,0:T(8,128)S(1)}, f32[2,80,128]{2,1,0:T(8,128)S(1)}, u32[]{:S(2)}, u32[]{:S(2)}) %collective-permute-start.16) | collective-permute-done | bytes 81952 | tf_op jit(solution)/shard_map/ppermute | solution.py:364
  79.3 2.9 %copy.16 = bf16[80,16,1024]{2,0,1:T(8,128)(2,1)} copy(bf16[80,16,1024]{2,1,0:T(8,128)(2,1)S(1)} %copy-done.1) | data formatting | bytes 5242880 | tf_op args[0]
  83.8 9.8 %batch.5 = (bf16[16,96,512]{2,1,0:T(8,128)(2,1)S(1)}, f32[2,80,128]{2,1,0:T(8,128)S(1)}) custom-call(f32[32,16]{1,0:T(8,128)S(1)} %get-tuple-element.37.refs_0_, bf16[256,16]{1,0:T(8,128)(2,1)S(1)} %fusion.refs_1_.order_ref, f32[8,80,128]{2,1,0:T(8,128)S(1)} %constant_dynamic-update-slice_fusion.4.refs_2_, ...), custom_call_target="tpu_custom_call" | custom-call | tf_op jit(solution)/shard_map/batch/pallas_call | solution.py:481
  93.6 2.3 %collective-permute-start.22 = (f32[2,80,128]{2,1,0:T(8,128)S(1)}, f32[2,80,128]{2,1,0:T(8,128)S(1)}, u32[]{:S(2)}, u32[]{:S(2)}) collective-permute-start(f32[2,80,128]{2,1,0:T(8,128)S(1)} %get-tuple-element.22), channel_id=1, source_target_pairs={{0,3},{1,2},{2,1},{3,0},{4,7},{5,6},{6,5},{7,4},{8,11},{9,10},{10,... | collective-permute-start | bytes 245768 | tf_op jit(solution)/shard_map/ppermute | solution.py:364
  96.0 2.1 %collective-permute-start.20 = (f32[2,80,128]{2,1,0:T(8,128)S(1)}, f32[2,80,128]{2,1,0:T(8,128)S(1)}, u32[]{:S(2)}, u32[]{:S(2)}) collective-permute-start(f32[2,80,128]{2,1,0:T(8,128)S(1)} %get-tuple-element.22), channel_id=1, source_target_pairs={{0,1},{1,0},{2,3},{3,2},{4,5},{5,4},{6,7},{7,6},{8,9},{9,8},{10,11... | collective-permute-start | bytes 245768 | tf_op jit(solution)/shard_map/ppermute | solution.py:364
  98.1 4.4 %collective-permute-done.20 = f32[2,80,128]{2,1,0:T(8,128)S(1)} collective-permute-done((f32[2,80,128]{2,1,0:T(8,128)S(1)}, f32[2,80,128]{2,1,0:T(8,128)S(1)}, u32[]{:S(2)}, u32[]{:S(2)}) %collective-permute-start.20) | collective-permute-done | bytes 81952 | tf_op jit(solution)/shard_map/ppermute | solution.py:364
  105.6 9.8 %last.1 = (f32[16,1024]{1,0:T(8,128)}, bf16[16,80,1024]{2,1,0:T(8,128)(2,1)S(1)}) custom-call(f32[32,16]{1,0:T(8,128)S(1)} %pad.4.pair_ref, bf16[256,16]{1,0:T(8,128)(2,1)S(1)} %fusion.refs_1_.order_ref, f32[8,80,128]{2,1,0:T(8,128)S(1)} %constant_dynamic-update-slice_fusion.8.own_ref, f32[8,80,128]{2,1,0:T(8,128)S(1)} %collective-permute-done.23.peer_ref, ...), custom_call_target="tpu_custom_call" | custom-call | tf_op jit(solution)/shard_map/last/pallas_call | solution.py:495
  115.4 2.9 %copy.14 = bf16[80,16,1024]{2,1,0:T(8,128)(2,1)} copy(bf16[80,16,1024]{2,0,1:T(8,128)(2,1)S(1)} %bitcast.48) | data formatting | bytes 5242880
  (90 shorter events, 19.8 us)
Async XLA Ops:
  1.4 16.7 %collective-permute-start = (f32[4,8,16]{2,1,0:T(8,128)S(1)}, f32[4,8,16]{2,1,0:T(8,128)S(1)}, u32[]{:S(2)}, u32[]{:S(2)}) collective-permute-start(f32[4,8,16]{2,1,0:T(8,128)S(1)} %convert_element_type.17), channel_id=1, source_target_pairs={{0,8},{8,0},{16,24},{24,16},{1,9},{9,1},{17,25},{25,17},{2,10},{10... | collective-permute-start | bytes 6152 | tf_op jit(solution)/shard_map/ppermute | solution.py:364
  8.9 6.6 %collective-permute-start.2 = (f32[2,80,128]{2,1,0:T(8,128)S(1)}, f32[2,80,128]{2,1,0:T(8,128)S(1)}, u32[]{:S(2)}, u32[]{:S(2)}) collective-permute-start(f32[2,80,128]{2,1,0:T(8,128)S(1)} %get-tuple-element.15), channel_id=1, source_target_pairs={{0,8},{8,0},{16,24},{24,16},{1,9},{9,1},{17,25},{25,17},{2,10},{10... | collective-permute-start | bytes 245768 | tf_op jit(solution)/shard_map/ppermute | solution.py:364
  14.7 8.6 %collective-permute-start.9 = (f32[3,88,256]{2,1,0:T(8,128)S(1)}, f32[3,88,256]{2,1,0:T(8,128)S(1)}, u32[]{:S(2)}, u32[]{:S(2)}) collective-permute-start(f32[3,88,256]{2,1,0:T(8,128)S(1)} %get-tuple-element.17), channel_id=1, source_target_pairs={{0,8},{8,0},{16,24},{24,16},{1,9},{9,1},{17,25},{25,17},{2,10},{10... | collective-permute-start | bytes 811016 | tf_op jit(solution)/shard_map/ppermute | solution.py:364
  15.5 5.9 %collective-permute-start.3 = (f32[2,80,128]{2,1,0:T(8,128)S(1)}, f32[2,80,128]{2,1,0:T(8,128)S(1)}, u32[]{:S(2)}, u32[]{:S(2)}) collective-permute-start(f32[2,80,128]{2,1,0:T(8,128)S(1)} %add.102), channel_id=1, source_target_pairs={{0,16},{8,24},{16,0},{24,8},{1,17},{9,25},{17,1},{25,9},{2,18},{10... | collective-permute-start | bytes 245768 | tf_op jit(solution)/shard_map/ppermute | solution.py:364
  18.1 12.5 %collective-permute-start.1 = (f32[4,16,16]{2,1,0:T(8,128)S(1)}, f32[4,16,16]{2,1,0:T(8,128)S(1)}, u32[]{:S(2)}, u32[]{:S(2)}) collective-permute-start(f32[4,16,16]{2,1,0:T(8,128)S(1)} %maximum_select_fusion.1), channel_id=1, source_target_pairs={{0,16},{8,24},{16,0},{24,8},{1,17},{9,25},{17,1},{25,9},{2,18},{10... | collective-permute-start | bytes 12296 | tf_op jit(solution)/shard_map/ppermute | solution.py:364
  21.4 4.5 %collective-permute-start.4 = (f32[2,80,128]{2,1,0:T(8,128)S(1)}, f32[2,80,128]{2,1,0:T(8,128)S(1)}, u32[]{:S(2)}, u32[]{:S(2)}) collective-permute-start(f32[2,80,128]{2,1,0:T(8,128)S(1)} %add.103), channel_id=1, source_target_pairs={{0,4},{4,0},{1,5},{5,1},{2,6},{6,2},{3,7},{7,3},{8,12},{12,8},{9,1... | collective-permute-start | bytes 245768 | tf_op jit(solution)/shard_map/ppermute | solution.py:364
  23.3 7.5 %collective-permute-start.10 = (f32[3,88,256]{2,1,0:T(8,128)S(1)}, f32[3,88,256]{2,1,0:T(8,128)S(1)}, u32[]{:S(2)}, u32[]{:S(2)}) collective-permute-start(f32[3,88,256]{2,1,0:T(8,128)S(1)} %add.105), channel_id=1, source_target_pairs={{0,16},{8,24},{16,0},{24,8},{1,17},{9,25},{17,1},{25,9},{2,18},{10... | collective-permute-start | bytes 811016 | tf_op jit(solution)/shard_map/ppermute | solution.py:364
  25.9 6.5 %collective-permute-start.7 = (f32[2,80,128]{2,1,0:T(8,128)S(1)}, f32[2,80,128]{2,1,0:T(8,128)S(1)}, u32[]{:S(2)}, u32[]{:S(2)}) collective-permute-start(f32[2,80,128]{2,1,0:T(8,128)S(1)} %add.104), channel_id=1, source_target_pairs={{0,3},{1,2},{2,1},{3,0},{4,7},{5,6},{6,5},{7,4},{8,11},{9,10},{10,... | collective-permute-start | bytes 245768 | tf_op jit(solution)/shard_map/ppermute | solution.py:364
  29.9 5.6 %collective-permute-start.6 = (f32[2,80,128]{2,1,0:T(8,128)S(1)}, f32[2,80,128]{2,1,0:T(8,128)S(1)}, u32[]{:S(2)}, u32[]{:S(2)}) collective-permute-start(f32[2,80,128]{2,1,0:T(8,128)S(1)} %add.104), channel_id=1, source_target_pairs={{0,2},{1,3},{2,0},{3,1},{4,6},{5,7},{6,4},{7,5},{8,10},{9,11},{10,... | collective-permute-start | bytes 245768 | tf_op jit(solution)/shard_map/ppermute | solution.py:364
  29.9 5.6 %collective-permute-start.5 = (f32[2,80,128]{2,1,0:T(8,128)S(1)}, f32[2,80,128]{2,1,0:T(8,128)S(1)}, u32[]{:S(2)}, u32[]{:S(2)}) collective-permute-start(f32[2,80,128]{2,1,0:T(8,128)S(1)} %add.104), channel_id=1, source_target_pairs={{0,1},{1,0},{2,3},{3,2},{4,5},{5,4},{6,7},{7,6},{8,9},{9,8},{10,11... | collective-permute-start | bytes 245768 | tf_op jit(solution)/shard_map/ppermute | solution.py:364
  30.9 6.6 %collective-permute-start.11 = (f32[3,88,256]{2,1,0:T(8,128)S(1)}, f32[3,88,256]{2,1,0:T(8,128)S(1)}, u32[]{:S(2)}, u32[]{:S(2)}) collective-permute-start(f32[3,88,256]{2,1,0:T(8,128)S(1)} %add.106), channel_id=1, source_target_pairs={{0,4},{4,0},{1,5},{5,1},{2,6},{6,2},{3,7},{7,3},{8,12},{12,8},{9,1... | collective-permute-start | bytes 811016 | tf_op jit(solution)/shard_map/ppermute | solution.py:364
  35.6 1.9 %collective-permute-start.8 = (f32[8,80,128]{2,1,0:T(8,128)S(1)}, f32[8,80,128]{2,1,0:T(8,128)S(1)}, u32[]{:S(2)}, u32[]{:S(2)}) collective-permute-start(f32[8,80,128]{2,1,0:T(8,128)S(1)} %pad_maximum_fusion.refs_2_), channel_id=1, source_target_pairs={{0,8},{8,0},{16,24},{24,16},{1,9},{9,1},{17,25},{25,17},{2,10},{10... | collective-permute-start | bytes 983048 | tf_op jit(solution)/shard_map/ppermute | solution.py:364
  46.3 10.5 %collective-permute-start.14 = (f32[2,80,128]{2,1,0:T(8,128)S(1)}, f32[2,80,128]{2,1,0:T(8,128)S(1)}, u32[]{:S(2)}, u32[]{:S(2)}) collective-permute-start(f32[2,80,128]{2,1,0:T(8,128)S(1)} %get-tuple-element.18), channel_id=1, source_target_pairs={{0,3},{1,2},{2,1},{3,0},{4,7},{5,6},{6,5},{7,4},{8,11},{9,10},{10,... | collective-permute-start | bytes 245768 | tf_op jit(solution)/shard_map/ppermute | solution.py:364
  49.9 6.8 %collective-permute-start.13 = (f32[2,80,128]{2,1,0:T(8,128)S(1)}, f32[2,80,128]{2,1,0:T(8,128)S(1)}, u32[]{:S(2)}, u32[]{:S(2)}) collective-permute-start(f32[2,80,128]{2,1,0:T(8,128)S(1)} %get-tuple-element.18), channel_id=1, source_target_pairs={{0,2},{1,3},{2,0},{3,1},{4,6},{5,7},{6,4},{7,5},{8,10},{9,11},{10,... | collective-permute-start | bytes 245768 | tf_op jit(solution)/shard_map/ppermute | solution.py:364
  49.9 4.7 %collective-permute-start.12 = (f32[2,80,128]{2,1,0:T(8,128)S(1)}, f32[2,80,128]{2,1,0:T(8,128)S(1)}, u32[]{:S(2)}, u32[]{:S(2)}) collective-permute-start(f32[2,80,128]{2,1,0:T(8,128)S(1)} %get-tuple-element.18), channel_id=1, source_target_pairs={{0,1},{1,0},{2,3},{3,2},{4,5},{5,4},{6,7},{7,6},{8,9},{9,8},{10,11... | collective-permute-start | bytes 245768 | tf_op jit(solution)/shard_map/ppermute | solution.py:364
  56.8 1.7 %collective-permute-start.15 = (f32[8,80,128]{2,1,0:T(8,128)S(1)}, f32[8,80,128]{2,1,0:T(8,128)S(1)}, u32[]{:S(2)}, u32[]{:S(2)}) collective-permute-start(f32[8,80,128]{2,1,0:T(8,128)S(1)} %constant_dynamic-update-slice_fusion.refs_2_), channel_id=1, source_target_pairs={{0,8},{8,0},{16,24},{24,16},{1,9},{9,1},{17,25},{25,17},{2,10},{10... | collective-permute-start | bytes 983048 | tf_op jit(solution)/shard_map/ppermute | solution.py:364
  69.4 9.8 %collective-permute-start.18 = (f32[2,80,128]{2,1,0:T(8,128)S(1)}, f32[2,80,128]{2,1,0:T(8,128)S(1)}, u32[]{:S(2)}, u32[]{:S(2)}) collective-permute-start(f32[2,80,128]{2,1,0:T(8,128)S(1)} %get-tuple-element.20), channel_id=1, source_target_pairs={{0,3},{1,2},{2,1},{3,0},{4,7},{5,6},{6,5},{7,4},{8,11},{9,10},{10,... | collective-permute-start | bytes 245768 | tf_op jit(solution)/shard_map/ppermute | solution.py:364
  71.7 7.5 %collective-permute-start.17 = (f32[2,80,128]{2,1,0:T(8,128)S(1)}, f32[2,80,128]{2,1,0:T(8,128)S(1)}, u32[]{:S(2)}, u32[]{:S(2)}) collective-permute-start(f32[2,80,128]{2,1,0:T(8,128)S(1)} %get-tuple-element.20), channel_id=1, source_target_pairs={{0,2},{1,3},{2,0},{3,1},{4,6},{5,7},{6,4},{7,5},{8,10},{9,11},{10,... | collective-permute-start | bytes 245768 | tf_op jit(solution)/shard_map/ppermute | solution.py:364
  71.7 6.6 %collective-permute-start.16 = (f32[2,80,128]{2,1,0:T(8,128)S(1)}, f32[2,80,128]{2,1,0:T(8,128)S(1)}, u32[]{:S(2)}, u32[]{:S(2)}) collective-permute-start(f32[2,80,128]{2,1,0:T(8,128)S(1)} %get-tuple-element.20), channel_id=1, source_target_pairs={{0,1},{1,0},{2,3},{3,2},{4,5},{5,4},{6,7},{7,6},{8,9},{9,8},{10,11... | collective-permute-start | bytes 245768 | tf_op jit(solution)/shard_map/ppermute | solution.py:364
  79.2 3.0 %collective-permute-start.19 = (f32[8,80,128]{2,1,0:T(8,128)S(1)}, f32[8,80,128]{2,1,0:T(8,128)S(1)}, u32[]{:S(2)}, u32[]{:S(2)}) collective-permute-start(f32[8,80,128]{2,1,0:T(8,128)S(1)} %constant_dynamic-update-slice_fusion.4.refs_2_), channel_id=1, source_target_pairs={{0,8},{8,0},{16,24},{24,16},{1,9},{9,1},{17,25},{25,17},{2,10},{10... | collective-permute-start | bytes 983048 | tf_op jit(solution)/shard_map/ppermute | solution.py:364
  93.6 10.2 %collective-permute-start.22 = (f32[2,80,128]{2,1,0:T(8,128)S(1)}, f32[2,80,128]{2,1,0:T(8,128)S(1)}, u32[]{:S(2)}, u32[]{:S(2)}) collective-permute-start(f32[2,80,128]{2,1,0:T(8,128)S(1)} %get-tuple-element.22), channel_id=1, source_target_pairs={{0,3},{1,2},{2,1},{3,0},{4,7},{5,6},{6,5},{7,4},{8,11},{9,10},{10,... | collective-permute-start | bytes 245768 | tf_op jit(solution)/shard_map/ppermute | solution.py:364
  96.0 7.9 %collective-permute-start.21 = (f32[2,80,128]{2,1,0:T(8,128)S(1)}, f32[2,80,128]{2,1,0:T(8,128)S(1)}, u32[]{:S(2)}, u32[]{:S(2)}) collective-permute-start(f32[2,80,128]{2,1,0:T(8,128)S(1)} %get-tuple-element.22), channel_id=1, source_target_pairs={{0,2},{1,3},{2,0},{3,1},{4,6},{5,7},{6,4},{7,5},{8,10},{9,11},{10,... | collective-permute-start | bytes 245768 | tf_op jit(solution)/shard_map/ppermute | solution.py:364
  96.0 6.6 %collective-permute-start.20 = (f32[2,80,128]{2,1,0:T(8,128)S(1)}, f32[2,80,128]{2,1,0:T(8,128)S(1)}, u32[]{:S(2)}, u32[]{:S(2)}) collective-permute-start(f32[2,80,128]{2,1,0:T(8,128)S(1)} %get-tuple-element.22), channel_id=1, source_target_pairs={{0,1},{1,0},{2,3},{3,2},{4,5},{5,4},{6,7},{7,6},{8,9},{9,8},{10,11... | collective-permute-start | bytes 245768 | tf_op jit(solution)/shard_map/ppermute | solution.py:364
  103.9 1.7 %collective-permute-start.23 = (f32[8,80,128]{2,1,0:T(8,128)S(1)}, f32[8,80,128]{2,1,0:T(8,128)S(1)}, u32[]{:S(2)}, u32[]{:S(2)}) collective-permute-start(f32[8,80,128]{2,1,0:T(8,128)S(1)} %constant_dynamic-update-slice_fusion.8.own_ref), channel_id=1, source_target_pairs={{0,8},{8,0},{16,24},{24,16},{1,9},{9,1},{17,25},{25,17},{2,10},{10... | collective-permute-start | bytes 983048 | tf_op jit(solution)/shard_map/ppermute | solution.py:364
  (7 other events, 98.6 us)
where the time goes:
time: 119 us; the launch traced here: 118 us
  Pallas kernels  45.8 us (38%)
  waiting for transfers between devices  29.1 us (24%)
  starting transfers between devices  27.1 us (23%)
  local copies, waits for them, and re-layouts  11.4 us (10%)
  other arithmetic  4.04 us (3%)
    ppermute x24, waiting for transfers between devices, swap(): lax.ppermute(x, axis, [(i, i ^ bit) for i in range(lax.axis_size(axis))])  29.1 us
    pallas_call x3, Pallas kernels, body(): pl.pallas_call(functools.partial(batch_kernel, index == 0), out_shape=(ja...  28.2 us
    ppermute x24, starting transfers between devices, swap(): lax.ppermute(x, axis, [(i, i ^ bit) for i in range(lax.axis_size(axis))])  27.1 us
    unnamed x25, local copies, waits for them, and re-layouts  11.2 us
    pallas_call x1, Pallas kernels, body(): pl.pallas_call(last_kernel, out_shape=(jax.ShapeDtypeStruct(background.sh...  9.77 us
    pallas_call x1, Pallas kernels, body(): pl.pallas_call(observe_kernel, grid=(batches - 1,), in_specs=[pl.BlockSpe...  5.72 us
  transfers between devices with their start and end apart: 24, of which 13 were waited for; matrix products, arithmetic and copies ran while one was open for 5% of the time, Pallas kernels for 7%

commit v1 on v0

v1 whole, which is shorter than its diff:
```python
import functools
import math

import jax
import jax.numpy as jnp
from jax import lax
from jax.experimental import pallas as pl
from jax.experimental.pallas import tpu as pltpu
from jax.sharding import PartitionSpec as P

F32 = jnp.float32
BF16 = jnp.bfloat16
LANES = 128
GROUP = 8
CHUNK = 32
DROWS = 96
VMEM_BYTES = 40 << 20
WHOLE_VMEM = 63 << 20


def params(limit=VMEM_BYTES):
    return pltpu.CompilerParams(vmem_limit_bytes=limit)


def split2(x):
    high = x.astype(BF16)
    return high, (x - high.astype(F32)).astype(BF16)


def nt_dot(a, b):
    return lax.dot_general(a, b, (((1,), (1,)), ((), ())), preferred_element_type=F32)


def observe_into(y_ref, hot_ref, pert_ref, mean_ref, local_cols, local_levs, ready=None):
    col_dev, count = hot_ref.shape
    lev_dev = mean_ref.shape[0]
    members = pert_ref.shape[0] // lev_dev
    for start in range(0, col_dev, 256):
        rows = lax.broadcasted_iota(jnp.int32, (256, count), 0) + start
        hot_ref[start : start + 256, :] = jnp.where(rows == local_cols, 1.0, 0.0).astype(BF16)
    lev_hot = lax.broadcasted_iota(jnp.int32, (lev_dev, count), 0) == local_levs
    hot = hot_ref[...]
    step = 16
    for start in range(0, members, step):
        if ready is not None:
            ready(start // step)
        picked = jnp.dot(
            pert_ref[start * lev_dev : (start + step) * lev_dev, :], hot, preferred_element_type=F32
        ).reshape(step, lev_dev, count)
        y_ref[start : start + step, :] = jnp.sum(jnp.where(lev_hot[None], picked, 0.0), axis=1)
    mean = mean_ref[...]
    high = mean.astype(BF16)
    rest = mean - high.astype(F32)
    middle = rest.astype(BF16)
    low = (rest - middle.astype(F32)).astype(BF16)
    picked = jnp.dot(jnp.concatenate([high, middle, low], axis=0), hot, preferred_element_type=F32)
    picked = (
        picked[:lev_dev] + picked[lev_dev : 2 * lev_dev] + picked[2 * lev_dev : 3 * lev_dev]
    )
    total = jnp.sum(jnp.where(lev_hot, picked, 0.0), axis=0, keepdims=True)
    tail = y_ref.shape[0] - members
    first = lax.broadcasted_iota(jnp.int32, (tail, count), 0) == 0
    y_ref[members:, :] = jnp.where(first, jnp.broadcast_to(total, (tail, count)), 0.0)


def half_first(x, core):
    half = x.shape[1] // 2
    return jnp.where(core == 0, x, jnp.concatenate([x[:, half:], x[:, :half]], axis=1))


def packed_grams(values, mean_row, sigma, vals, members):
    root = math.sqrt(members - 1.0)
    count = values.shape[1]
    scale = 1.0 / (sigma * root)
    innov = (vals - mean_row) / sigma
    wide = values.astype(F32) * (scale * scale)
    pad = LANES - members
    first = lax.broadcasted_iota(jnp.int32, (pad, count), 0) == 0
    last = jnp.where(first, jnp.broadcast_to(scale * innov, (pad, count)), 0.0)
    high, low = split2(jnp.concatenate([wide, last], axis=0))
    row = lax.broadcasted_iota(jnp.int32, (members, LANES), 0)
    lane = tile_lanes((members, LANES))
    results = []
    for start in range(0, count, 2 * LANES):
        grams = []
        for at in (slice(start, start + LANES), slice(start + LANES, start + 2 * LANES)):
            left = jnp.concatenate([values[:, at], values[:, at]], axis=1)
            right = jnp.concatenate([high[:, at], low[:, at]], axis=1)
            grams.append(nt_dot(left, right))
        a, b = grams
        diagonal = jnp.sum(jnp.where(lane == row, b, 0.0), axis=1, keepdims=True)
        packed = jnp.where((lane <= row) | (lane == members), a, jnp.where(lane < members, b, 0.0))
        packed = jnp.where(lane == members + 1, b[:, members : members + 1], packed)
        results.append(jnp.where(lane == members + 2, diagonal, packed))
    return results


def unpack_into(full_ref, refs, members):
    row = lax.broadcasted_iota(jnp.int32, (members, LANES), 0)
    lane = tile_lanes((members, LANES))
    index = 0
    for ref in refs:
        for block in range(ref.shape[0]):
            packed = ref[block]
            square = jnp.concatenate([packed, jnp.zeros((LANES - members, LANES), F32)], axis=0)
            turned = square.T[:members]
            full_ref[index] = jnp.where(
                (lane <= row) | (lane == members), packed, jnp.where(lane < members, turned, 0.0)
            )
            other = jnp.where(lane == row, packed[:, members + 2 : members + 3], jnp.where(lane < row, turned, packed))
            full_ref[index + 1] = jnp.where(
                lane < members, other, jnp.where(lane == members, packed[:, members + 1 : members + 2], 0.0)
            )
            index += 2


def observe_batch(y_ref, hot_ref, pert_ref, mean_ref, cols_ref, levs_ref, batch, ready=None):
    core = lax.axis_index("cols") % 2
    col_dev, lev_dev = hot_ref.shape[0], mean_ref.shape[0]
    cols = half_first(cols_ref[batch : batch + 1, :], core) - lax.axis_index("cols") * col_dev
    levs = half_first(levs_ref[batch : batch + 1, :], core) - lax.axis_index("levs") * lev_dev
    observe_into(y_ref, hot_ref, pert_ref, mean_ref, cols, levs, ready)


def store_blocks(y_ref, keep_refs, send_refs):
    for block, ref in enumerate((*keep_refs, *send_refs)):
        ref[...] = y_ref[:, block * LANES : (block + 1) * LANES]


def fetch(sources, held, sems, pert_sems):
    pert_ref, mean_ref = held[:2]
    small = [pltpu.make_async_copy(sources[i], held[i], sems.at[i - 1]) for i in range(1, len(held))]
    step = 16 * mean_ref.shape[0]
    large = [
        pltpu.make_async_copy(sources[0].at[start : start + step, :], pert_ref.at[start : start + step, :], pert_sems.at[i])
        for i, start in enumerate(range(0, pert_ref.shape[0], step))
    ]
    for copy in small + large:
        copy.start()
    for copy in small:
        copy.wait()
    return large


def fetch_scratch(sources, members):
    return [pltpu.VMEM(x.shape, x.dtype) for x in sources] + [
        pltpu.SemaphoreType.DMA((len(sources) - 1,)),
        pltpu.SemaphoreType.DMA((members // 16,)),
    ]


def first_kernel(*refs):
    sources, (keep_ref, send_ref), scratch = refs[:7], refs[7:9], refs[9:]
    held, (sems, pert_sems, y_ref, hot_ref) = scratch[:7], scratch[7:]
    pert_ref, mean_ref, cols_ref, levs_ref, sigma_ref, vals_ref, pair_ref = held
    large = fetch(sources, held, sems, pert_sems)
    core = lax.axis_index("cols") % 2
    members = pert_ref.shape[0] // mean_ref.shape[0]
    batches, tiles_dev, block_count = pair_ref.shape
    observe_batch(y_ref, hot_ref, pert_ref, mean_ref, cols_ref, levs_ref, 0, lambda i: large[i].wait())
    grams = packed_grams(
        y_ref[:members, :].astype(BF16),
        y_ref[members : members + 1, :],
        half_first(sigma_ref[0:1, :], core),
        half_first(vals_ref[0:1, :], core),
        members,
    )
    cols_size = lax.axis_size("cols")
    extra = batches * cols_size
    spread = jnp.where(
        tile_lanes((block_count, LANES)) % block_count == lax.broadcasted_iota(jnp.int32, (block_count, LANES), 0), 1.0, 0.0
    ).astype(BF16)
    mine = tile_lanes((tiles_dev, LANES)) // block_count == lax.broadcasted_iota(jnp.int32, (tiles_dev, LANES), 0)
    row = lax.broadcasted_iota(jnp.int32, (extra, LANES), 0)
    total = jnp.zeros((extra, LANES), F32)
    for batch in range(batches):
        wide = jnp.dot(pair_ref[batch].astype(F32).astype(BF16), spread, preferred_element_type=F32)
        line = jnp.sum(jnp.where(mine, wide, 0.0), axis=0, keepdims=True)
        total = jnp.where(row == batch * cols_size + lax.axis_index("cols"), line, total)
    total = jnp.where(lax.axis_index("levs") == 0, total, 0.0)
    for ref, gram in zip((keep_ref, send_ref), grams):
        ref[:members, :] = gram
        ref[members : members + extra, :] = total
    observe_batch(y_ref, hot_ref, pert_ref, mean_ref, cols_ref, levs_ref, 1)
    rows = y_ref.shape[0]
    places = range(members + extra, keep_ref.shape[0], rows)
    store_blocks(y_ref, *[[ref.at[place : place + rows, :] for place in places] for ref in (keep_ref, send_ref)])


def observe_kernel(batches, pert_ref, mean_ref, cols_ref, levs_ref, keep_ref, send_ref, y_ref, hot_ref):
    per = keep_ref.shape[0] // len(batches)
    for index, batch in enumerate(batches):
        observe_batch(y_ref, hot_ref, pert_ref, mean_ref, cols_ref, levs_ref, batch)
        store_blocks(y_ref, [keep_ref.at[index * per + i] for i in range(per)], [send_ref.at[index * per + i] for i in range(per)])


def tile_lanes(shape):
    return lax.broadcasted_iota(jnp.int32, shape, 1)


def block_order(block_count, own_blocks):
    place = lax.broadcasted_iota(jnp.int32, (2 * block_count * GROUP, LANES), 0) // GROUP % block_count
    side, rest = place // (block_count // 2), place % (block_count // 2)
    hop, block = rest // own_blocks, rest % own_blocks
    core = lax.axis_index("cols") % 2
    wanted = (lax.axis_index("owner") ^ hop) * (2 * own_blocks) + (core ^ side) * own_blocks + block
    return jnp.where(wanted == lax.broadcasted_iota(jnp.int32, wanted.shape, 1) % block_count, 1.0, 0.0).astype(BF16)


def pair_rows(lines, block_count):
    per = LANES // block_count
    rows = jnp.concatenate(
        [jnp.broadcast_to(lines[i : i + 1, :], (per, LANES)) for i in range(lines.shape[0])], axis=0
    )
    row = lax.broadcasted_iota(jnp.int32, rows.shape, 0)
    return jnp.where(tile_lanes(rows.shape) // block_count == row % per, rows, 0.0)


def build_systems(s_ref, pairs, full_ref):
    members = full_ref.shape[1]
    chunk = pairs.shape[0]
    pack = LANES // chunk
    order = block_order(full_ref.shape[0], 2)
    width = GROUP * chunk
    spread = nt_dot(order, jnp.concatenate([pairs.astype(BF16)] * (max(width, LANES) // chunk), axis=0))
    row = lax.broadcasted_iota(jnp.int32, spread.shape, 0)
    lane = tile_lanes(spread.shape)
    sides = max(1, LANES // width)
    select = jnp.concatenate(
        [jnp.where(row % GROUP + side * GROUP == lane // chunk, spread, 0.0) for side in range(sides)], axis=0
    ).astype(BF16)
    rows = s_ref.shape[1]
    out_row = lax.broadcasted_iota(jnp.int32, (rows, LANES), 0)
    out_pack = tile_lanes((rows, LANES)) // chunk
    for start in range(0, members, GROUP * sides):
        parts = []
        for side in range(sides):
            at = slice(start + side * GROUP, start + (side + 1) * GROUP)
            stacked = jnp.concatenate([full_ref[block, at, :] for block in range(full_ref.shape[0])], axis=0)
            parts.extend(split2(stacked.T[:rows]))
        product = jnp.dot(jnp.concatenate(parts, axis=1), select, preferred_element_type=F32)
        for part in range(product.shape[1] // LANES):
            first = start + part * pack
            s_ref[first // pack] = product[:, part * LANES : (part + 1) * LANES] + jnp.where(
                out_row == first + out_pack, 1.0, 0.0
            )


def invert_factors(s_ref, r_ref, m_ref, wrow_ref, members):
    one = jnp.where(
        lax.broadcasted_iota(jnp.int32, (LANES, LANES), 0) == tile_lanes((LANES, LANES)), 1.0, 0.0
    ).astype(BF16)
    pad = jnp.zeros((LANES - members, LANES), F32)
    rows = s_ref.shape[1]
    chunk = wrow_ref.shape[0]
    pack_size = LANES // chunk
    pack = tile_lanes((GROUP, LANES)) // chunk
    within = tile_lanes((rows, LANES)) % chunk
    group_row = lax.broadcasted_iota(jnp.int32, (GROUP, LANES), 0)
    count = members // GROUP
    weights = [jnp.zeros((GROUP, LANES), F32) for _ in range(count)]
    picks = [within + p * chunk for p in range(pack_size)]
    share = min(pack_size, GROUP)
    for s in range(count):
        start = s * GROUP
        first = start // pack_size
        inner = start % pack_size
        copies = []
        for a in range(GROUP):
            copies.append(jnp.take_along_axis(s_ref[first + a // share], picks[inner + a % share], axis=1))
        entry = [[None] * GROUP for _ in range(GROUP)]
        for a in range(GROUP):
            for b in range(a, GROUP):
                entry[a][b] = jnp.broadcast_to(copies[a][start + b : start + b + 1, :], (GROUP, LANES))
        ratio = [[None] * GROUP for _ in range(GROUP)]
        inverse = [None] * GROUP
        for a in range(GROUP):
            inverse[a] = 1.0 / entry[a][a]
            for b in range(a + 1, GROUP):
                ratio[b][a] = entry[a][b] * inverse[a]
            for b in range(a + 1, GROUP):
                for c in range(b, GROUP):
                    entry[b][c] = entry[b][c] - ratio[b][a] * entry[a][c]
        roots = [lax.rsqrt(entry[a][a]) for a in range(GROUP)]
        pieces = rows // GROUP
        lower = [[None] * pieces for _ in range(GROUP)]
        for v in range(pieces):
            for a in range(GROUP):
                if v == s:
                    value = jnp.where(group_row == a, 1.0, 0.0)
                else:
                    value = copies[a][v * GROUP : (v + 1) * GROUP, :]
                for b in range(a):
                    value = value - ratio[a][b] * lower[b][v]
                lower[a][v] = value
        more = start + GROUP < members
        if more:
            for v in range(pieces):
                solved = [None] * GROUP
                for a in range(GROUP - 1, -1, -1):
                    value = lower[a][v] * inverse[a]
                    for b in range(a + 1, GROUP):
                        value = value - ratio[b][a] * solved[b]
                    solved[a] = value
                for a in range(GROUP):
                    value = solved[a]
                    if v == s:
                        value = value + jnp.where(group_row == a, 1.0, 0.0)
                    r_ref[a, v * GROUP : (v + 1) * GROUP, :] = value
        for part in range(GROUP // share):

            def merged(v):
                value = lower[part * share][v] * roots[part * share]
                for p in range(1, share):
                    a = part * share + p
                    value = jnp.where(pack == inner + p, lower[a][v] * roots[a], value)
                return value

            halfway = jnp.broadcast_to(merged(count)[0:1, :], (GROUP, LANES))
            finished = [merged(v) for v in range(s + 1)]
            valid = (pack >= inner) & (pack < inner + share)
            for v in range(s + 1):
                weights[v] = weights[v] + jnp.where(valid, halfway * finished[v], 0.0)
            finished += [jnp.zeros((GROUP, LANES), F32)] * (count - 1 - s)
            block = first + part
            turned = nt_dot(one, jnp.concatenate(finished + [pad], axis=0).astype(BF16))
            at = inner * chunk
            m_ref[block * LANES + at : block * LANES + at + share * chunk, :] = turned[at : at + share * chunk]
        if more:

            def update(block, masked, start=start, inner=inner):
                old = s_ref[block, start : start + GROUP, :]
                if masked:
                    old = jnp.where(pack >= inner + GROUP, old, 0.0)
                factors = [jnp.broadcast_to(old[a : a + 1, :], (GROUP, LANES)) for a in range(GROUP)]
                for v in range(pieces):
                    at = slice(v * GROUP, (v + 1) * GROUP)
                    value = s_ref[block, at, :]
                    for a in range(GROUP):
                        value = value - factors[a] * r_ref[a, at, :]
                    s_ref[block, at, :] = value

            if pack_size > GROUP:
                if inner + GROUP < pack_size:
                    update(first, True)
                for block in range(first + 1, s_ref.shape[0]):
                    update(block, False)
            else:
                per = GROUP // pack_size

                def trailing(index, carry, first=first, update=update, per=per):
                    for step in range(per):
                        update(first + (index + 1) * per + step, False)
                    return carry

                trips = count - 1 - s
                lax.fori_loop(0, trips, trailing, 0, unroll=max(d for d in (1, 2, 3) if trips % d == 0))
    for v in range(count):
        shift = chunk
        while shift < LANES:
            weights[v] = weights[v] + pltpu.roll(weights[v], shift, 1)
            shift *= 2
    wrow_ref[...] = nt_dot(one[:chunk], jnp.concatenate(weights + [pad], axis=0).astype(BF16))


def factor_chunk(pairs, s_ref, r_ref, m_ref, wrow_ref, full_ref):
    build_systems(s_ref, pairs, full_ref)
    invert_factors(s_ref, r_ref, m_ref, wrow_ref, full_ref.shape[1])


def factor_scratch(members, block_count, chunk):
    return [
        pltpu.VMEM((members * chunk // LANES, members + GROUP, LANES), F32),
        pltpu.VMEM((GROUP, members + GROUP, LANES), F32),
        pltpu.VMEM((members * chunk, LANES), F32),
        pltpu.VMEM((chunk, LANES), F32),
        pltpu.VMEM((block_count, members, LANES), F32),
    ]


def product_of(m_ref, w_ref, tile, old, members):
    rows = m_ref[pl.ds(tile, members, stride=w_ref.shape[0]), :].astype(BF16)
    tail = DROWS - members
    sub = lax.broadcasted_iota(jnp.int32, (tail, LANES), 0)
    lane = lax.broadcasted_iota(jnp.int32, (tail, LANES), 1)
    weights = jnp.broadcast_to(w_ref[pl.ds(tile, 1), :], (tail, LANES))
    if old is None:
        return jnp.concatenate([rows, jnp.where(sub == 0, weights, 0.0).astype(BF16)], axis=0), None
    ones = (lane >= members) & (lane < members + 2)
    extra = jnp.where(sub == 0, jnp.where(ones, 1.0, weights), 0.0).astype(BF16)
    left = jnp.concatenate([rows, extra], axis=0)[:, :DROWS]
    new = jnp.dot(left, old[0], preferred_element_type=F32)
    if old[1] is not None:
        new = new + jnp.dot(left, old[1], preferred_element_type=F32)
    total = jnp.broadcast_to(new[members : members + 1, :], (tail, LANES))
    high = total.astype(BF16).astype(F32)
    last = jnp.where(sub == 0, high, jnp.where(sub == 1, total - high, 0.0))
    return split2(jnp.concatenate([new[:members], last], axis=0))


def products(m_ref, w_ref, old_ref, new_ref, base, pairs_of, members, old_base=None):
    old_base = base if old_base is None else old_base

    def pair(index, carry):
        for side in range(2):
            at = slice(side * LANES, (side + 1) * LANES)
            low_at = slice((side + 2) * LANES, (side + 3) * LANES)
            old = None
            if old_ref is not None:
                old = old_ref[old_base + index, :, at], None
                if old_ref.shape[2] > 2 * LANES:
                    old = old[0], old_ref[old_base + index, :, low_at]
            high, low = product_of(m_ref, w_ref, index * 2 + side, old, members)
            new_ref[base + index, :, at] = high
            if low is not None:
                new_ref[base + index, :, low_at] = low
        return carry

    lax.fori_loop(0, pairs_of, pair, 0, unroll=2)


def factor_part(index, total_ref, own_ref, peer_ref, old_ref, new_ref, factor):
    members = own_ref.shape[1]
    block_count = factor[4].shape[0]
    cols_size = lax.axis_size("cols")
    unpack_into(factor[4], (own_ref, peer_ref), members)
    lines = CHUNK * block_count // LANES
    chunks = cols_size // lines

    def one_chunk(chunk):
        rows = total_ref[pl.ds(members + index * cols_size + chunk * lines, lines), :]
        factor_chunk(pair_rows(rows, block_count), *factor)
        products(factor[2], factor[3], old_ref, new_ref, chunk * (CHUNK // 2), CHUNK // 2, members)

    if chunks == 1:
        one_chunk(0)
    else:
        pl.loop(0, chunks)(one_chunk)


def moments_part(index, y, cols_ref, sigma_ref, vals_ref, new_ref, gram_ref, x_ref):
    members = gram_ref.shape[0]
    root = math.sqrt(members - 1.0)
    core = lax.axis_index("cols") % 2
    count = x_ref.shape[1]
    later = slice(index + 1, index + 2)
    tile = half_first(cols_ref[later, :], core)[:, :count] // LANES
    y = jnp.concatenate(y, axis=1)
    start_values = y[:members, :]
    empty = jnp.zeros((LANES - members, count), BF16)
    for side in range(2):
        x_ref[side * LANES : side * LANES + members, :] = jnp.where(tile % 2 == side, start_values, 0.0).astype(BF16)
        x_ref[side * LANES + members : (side + 1) * LANES, :] = empty
    parts = new_ref.shape[2] // (2 * LANES)
    stacked = jnp.concatenate([x_ref[...]] * parts, axis=0)
    half_tile = tile // 2
    per = 4

    def gather(index, total):
        at = new_ref[pl.ds(index * per, per)].reshape(per * DROWS, new_ref.shape[2])
        product = jnp.dot(at, stacked, preferred_element_type=F32)
        for k in range(per):
            total = jnp.where(half_tile == index * per + k, product[k * DROWS : (k + 1) * DROWS], total)
        return total

    now = lax.fori_loop(0, new_ref.shape[0] // per, gather, jnp.zeros((DROWS, count), F32))
    mean_row = y[members : members + 1, :] + (now[members : members + 1] + now[members + 1 : members + 2]) / root
    gram_ref[...] = packed_grams(
        now[:members].astype(BF16),
        mean_row,
        half_first(sigma_ref[later, :], core)[:, :count],
        half_first(vals_ref[later, :], core)[:, :count],
        members,
    )[0]


def batch_kernel(index, total_ref, own_ref, peer_ref, *refs):
    old_ref, y_ref = refs[:2] if index else (None, None)
    cols_ref, sigma_ref, vals_ref, new_ref, gram_ref, x_ref, *factor = refs[2 if index else 0 :]
    members = own_ref.shape[1]
    factor_part(index, total_ref, own_ref, peer_ref, old_ref, new_ref, factor)
    blocks = x_ref.shape[1] // LANES
    if index:
        y = [y_ref[(index - 1) * blocks + block] for block in range(blocks)]
    else:
        rows = members + GROUP
        places = range(total_ref.shape[0] - blocks * rows, total_ref.shape[0], rows)
        y = [total_ref[place : place + rows, :] for place in places]
    moments_part(index, y, cols_ref, sigma_ref, vals_ref, new_ref, gram_ref, x_ref)


def last_kernel(batches, total_ref, own_ref, peer_ref, old_ref, pert_ref, mean_ref, out_mean_ref, out_ref, new_ref, *factor):
    members = own_ref.shape[1]
    root = math.sqrt(members - 1.0)
    tiles = new_ref.shape[0] * 2
    unpack_into(factor[4], (own_ref, peer_ref), members)
    cols_size = lax.axis_size("cols")
    line = total_ref[pl.ds(members + (batches - 1) * cols_size + lax.axis_index("cols"), 1), :]
    pairs = pair_rows(line, factor[4].shape[0])
    factor_chunk(pairs, *factor)
    own_first = lax.axis_index("cols") * new_ref.shape[0]
    products(factor[2], factor[3], old_ref, new_ref, 0, new_ref.shape[0], members, own_first)
    width = pert_ref.shape[2] // tiles
    levs = pert_ref.shape[0]
    step = 16
    turn_shape = (step * levs, step * levs)
    turn_row = lax.broadcasted_iota(jnp.int32, turn_shape, 0)
    source = turn_row % levs * step + turn_row // levs
    turn = jnp.where(lax.broadcasted_iota(jnp.int32, turn_shape, 1) == source, 1.0, 0.0).astype(BF16)
    for pair in range(tiles // 2):
        news = [[] for _ in range(levs)]
        for side in range(2):
            left = new_ref[pair, :, side * LANES : side * LANES + members]
            left_low = new_ref[pair, :, (side + 2) * LANES : (side + 2) * LANES + members]
            at = slice((pair * 2 + side) * width, (pair * 2 + side + 1) * width)
            for lev in range(levs):
                pert = pert_ref[lev, :, at]
                new = jnp.dot(left, pert, preferred_element_type=F32) + jnp.dot(
                    left_low, pert, preferred_element_type=F32
                )
                gain = new[members : members + 1] + new[members + 1 : members + 2]
                out_mean_ref[lev : lev + 1, at] = mean_ref[lev : lev + 1, at] + gain / root
                news[lev].append(new[:members].astype(BF16))
        news = [jnp.concatenate(sides, axis=1) for sides in news]
        at = slice(pair * 2 * width, (pair + 1) * 2 * width)
        for start in range(0, members, step):
            block = jnp.concatenate([new[start : start + step] for new in news], axis=0)
            turned = jnp.dot(turn, block, preferred_element_type=F32).astype(BF16)
            out_ref[start * levs : (start + step) * levs, at] = turned


def swap(x, axis, bit):
    return lax.ppermute(x, axis, [(i, i ^ bit) for i in range(lax.axis_size(axis))])


def upper_bits(axis, first):
    bit, bits = first, []
    while bit < lax.axis_size(axis):
        bits.append(bit)
        bit *= 2
    return bits


def after(x, *others):
    return lax.optimization_barrier((x, *others))[0]


def body(perturbations, background, obs_cols, obs_levs, obs_vals, obs_sigma, pairs):
    members, lev_dev, col_dev = perturbations.shape
    batches, obs_own = obs_cols.shape
    tiles_dev, block_count = pairs.shape[1:]
    cols_size, owners = lax.axis_size("cols"), lax.axis_size("owner")
    tiles = tiles_dev * cols_size
    half = obs_own // 2
    blocks = half // LANES
    assert block_count // owners // 2 == blocks == 2
    assert col_dev == tiles_dev * LANES == LANES * LANES // block_count

    flat = perturbations.reshape(members * lev_dev, col_dev)
    rows = members + GROUP
    observed_scratch = [pltpu.VMEM((rows, obs_own), F32), pltpu.VMEM((col_dev, obs_own), BF16)]
    message = jax.ShapeDtypeStruct((members + batches * cols_size + blocks * rows, LANES), F32)
    sources = (flat, background, obs_cols, obs_levs, obs_sigma, obs_vals, pairs)
    keep, send = pl.pallas_call(
        first_kernel,
        in_specs=[pl.BlockSpec(memory_space=pltpu.MemorySpace.HBM)] * len(sources),
        out_shape=(message, message),
        scratch_shapes=fetch_scratch(sources, members) + observed_scratch,
        compiler_params=params(WHOLE_VMEM),
        name="first",
    )(*sources)

    def observe(which, obs_cols):
        shape = jax.ShapeDtypeStruct((blocks * len(which), rows, LANES), F32)
        return pl.pallas_call(
            functools.partial(observe_kernel, which),
            out_shape=(shape, shape),
            scratch_shapes=observed_scratch,
            compiler_params=params(),
            cost_estimate=pl.CostEstimate(flops=2 * 10**9 * len(which), bytes_accessed=10**7, transcendentals=0),
            name="observe",
        )(flat, background, obs_cols, obs_levs)

    stages = [("cols", bit) for bit in upper_bits("cols", 2)] + [("levs", bit) for bit in upper_bits("levs", 1)]
    total = keep + swap(send, "cols", 1)
    for axis, bit in stages:
        total = total + swap(total, axis, bit)
    gram_own = total[:members]

    def spread(gram_own):
        own = jnp.stack([gram_own] + [swap(gram_own, "owner", hop) for hop in range(1, owners)])
        return own, swap(own, "cols", 1)

    product = None
    for index in range(batches - 1):
        if index == 0:
            y_keep, y_send = observe(tuple(range(2, batches)), after(obs_cols, gram_own))
        own, peer = spread(gram_own)
        if index == 0:
            own = after(own, y_keep)
            y_later = y_keep + swap(y_send, "cols", 1)
            for axis, bit in stages:
                y_later = y_later + swap(y_later, axis, bit)
        if index == 1:
            by_level = jnp.transpose(after(perturbations, gram_own), (1, 0, 2))
            own = after(own, by_level)
        product, gram_own = pl.pallas_call(
            functools.partial(batch_kernel, index),
            out_shape=(
                jax.ShapeDtypeStruct((tiles // 2, DROWS, (4 if index else 2) * LANES), BF16),
                jax.ShapeDtypeStruct((members, LANES), F32),
            ),
            scratch_shapes=[pltpu.VMEM((2 * LANES, half), BF16), *factor_scratch(members, block_count, CHUNK)],
            compiler_params=params(),
            cost_estimate=pl.CostEstimate(flops=10**10, bytes_accessed=10**7, transcendentals=0),
            name="batch",
        )(total, own, peer, *((product, y_later) if index else ()), obs_cols, obs_sigma, obs_vals)

    own, peer = spread(gram_own)
    pairs_of = tiles_dev // 2
    mean, out = pl.pallas_call(
        functools.partial(last_kernel, batches),
        out_shape=(
            jax.ShapeDtypeStruct(background.shape, F32),
            jax.ShapeDtypeStruct(flat.shape, BF16),
        ),
        scratch_shapes=[
            pltpu.VMEM((pairs_of, DROWS, 4 * LANES), BF16),
            *factor_scratch(members, block_count, tiles_dev),
        ],
        compiler_params=params(),
        name="last",
    )(total, own, peer, product, by_level, background)
    return mean, out.reshape(perturbations.shape)


def solution(mesh):
    return jax.shard_map(
        body,
        mesh=mesh,
        in_specs=(
            P(None, "levs", "cols"),
            P("levs", "cols"),
            P(None, "owner"),
            P(None, "owner"),
            P(None, "owner"),
            P(None, "owner"),
            P(None, "cols", None),
        ),
        out_specs=(P("levs", "cols"), P(None, "levs", "cols")),
        check_vma=False,
    )
```

time: 119 us -> 104 us (0.87)
  local copies, waits for them, and re-layouts: 11.4 us -> 3.21 us
  waiting for transfers between devices: 29.1 us -> 21.6 us
  Pallas kernels: 45.8 us -> 49.5 us
  other arithmetic: 4.04 us -> 1.08 us
    unnamed x25 -> x14, local copies, waits for them, and re-layouts: 11.2 us -> 1.77 us
    ppermute x24 -> x22, waiting for transfers between devices: 29.1 us -> 21.6 us  [swap(): lax.ppermute(x, axis, [(i, i ^ bit) for i in range(lax.axis_size(axis))])]
    pallas_call x6, Pallas kernels: 45.8 us -> 49.5 us  [the longest x3 29 us: body(): pl.pallas_call(functools.partial(batch_kernel, index), out_shape=(jax.Sha...]
    sub x2 -> x0, other arithmetic: 1.55 us -> none  [the longest x1 0.78 us: body(): local_cols = (cols_half - cols_index * col_dev).reshape(batches, 1, obs_own)]
    convert_element_type x3 -> x0, other arithmetic: 1.51 us -> none  [the longest x1 0.72 us: body(): all_pairs = pairs.astype(F32)]
    optimization_barrier x0 -> x1, local copies, waits for them, and re-layouts: none -> 1.44 us  [after(): return lax.optimization_barrier((x, *others))[0]]
    ppermute x24 -> x22, starting transfers between devices: 27.1 us -> 27.1 us  [swap(): lax.ppermute(x, axis, [(i, i ^ bit) for i in range(lax.axis_size(axis))])]
  transfers between devices with their start and end apart: 24 -> 22, of which waited for: 13 -> 12; matrix products, arithmetic and copies ran while one was open for 5% -> 1% of each run, Pallas kernels for 7% -> 12%
where the time goes in v1:
time: 104 us; the launch traced here: 103 us
  Pallas kernels  49.5 us (48%)
  starting transfers between devices  27.1 us (26%)
  waiting for transfers between devices  21.6 us (21%)
  local copies, waits for them, and re-layouts  3.21 us (3%)
  other arithmetic  1.08 us (1%)
    pallas_call x3, Pallas kernels, body(): pl.pallas_call(functools.partial(batch_kernel, index), out_shape=(jax.Sha...  29 us
    ppermute x22, starting transfers between devices, swap(): lax.ppermute(x, axis, [(i, i ^ bit) for i in range(lax.axis_size(axis))])  27.1 us
    ppermute x22, waiting for transfers between devices, swap(): lax.ppermute(x, axis, [(i, i ^ bit) for i in range(lax.axis_size(axis))])  21.6 us
    pallas_call x1, Pallas kernels, body(): pl.pallas_call(functools.partial(last_kernel, batches), out_shape=(jax.Sh...  9.98 us
    pallas_call x1, Pallas kernels, body(): pl.pallas_call(first_kernel, in_specs=[pl.BlockSpec(memory_space=pltpu.Me...  6.87 us
    pallas_call x1, Pallas kernels, observe(): pl.pallas_call(functools.partial(observe_kernel, which), out_shape=(shape...  3.73 us
  transfers between devices with their start and end apart: 22, of which 12 were waited for; matrix products, arithmetic and copies ran while one was open for 1% of the time, Pallas kernels for 12%

profile of v1, /device:TPU:0, one launch (start us, length us, event | category | flops | bytes accessed | tf_op | source)
XLA Modules:
  0.0 103.4 jit_solution(3288222270398075983)
XLA Ops:
  0.7 6.9 %first.1 = (f32[272,128]{1,0:T(8,128)}, f32[272,128]{1,0:T(8,128)}) custom-call(bf16[1280,1024]{1,0:T(8,128)(2,1)} %bitcast.22, f32[16,1024]{1,0:T(8,128)} %mean_ref.3, s32[4,512]{1,0:T(4,128)} %refs_2_.7, s32[4,512]{1,0:T(4,128)} %levs_ref.1, f32[4,512]{1,0:T(4,128)} %refs_3_.5, f32[4,512]{1,0:T(4,128)} %refs_4_.5, s32[4,8,16]{2,1,0:T(8,128)} %refs_6_.1), custom_call_target="tpu_custom_call" | custom-call | tf_op jit(solution)/shard_map/first/pallas_call | solution.py:564
  10.2 2.9 %collective-permute-start.1 = (f32[272,128]{1,0:T(8,128)S(1)}, f32[272,128]{1,0:T(8,128)S(1)}, u32[]{:S(2)}, u32[]{:S(2)}) collective-permute-start(f32[272,128]{1,0:T(8,128)S(1)} %add.18), channel_id=1, source_target_pairs={{0,16},{8,24},{16,0},{24,8},{1,17},{9,25},{17,1},{25,9},{2,18},{10... | collective-permute-start | bytes 417800 | tf_op jit(solution)/shard_map/ppermute | solution.py:533
  13.1 4.0 %collective-permute-done.1 = f32[272,128]{1,0:T(8,128)S(1)} collective-permute-done((f32[272,128]{1,0:T(8,128)S(1)}, f32[272,128]{1,0:T(8,128)S(1)}, u32[]{:S(2)}, u32[]{:S(2)}) %collective-permute-start.1) | collective-permute-done | bytes 139296 | tf_op jit(solution)/shard_map/ppermute | solution.py:533
  17.1 1.8 %collective-permute-start.2 = (f32[272,128]{1,0:T(8,128)S(1)}, f32[272,128]{1,0:T(8,128)S(1)}, u32[]{:S(2)}, u32[]{:S(2)}) collective-permute-start(f32[272,128]{1,0:T(8,128)S(1)} %add.19), channel_id=1, source_target_pairs={{0,4},{4,0},{1,5},{5,1},{2,6},{6,2},{3,7},{7,3},{8,12},{12,8},{9,1... | collective-permute-start | bytes 417800 | tf_op jit(solution)/shard_map/ppermute | solution.py:533
  18.9 3.5 %collective-permute-done.2 = f32[272,128]{1,0:T(8,128)S(1)} collective-permute-done((f32[272,128]{1,0:T(8,128)S(1)}, f32[272,128]{1,0:T(8,128)S(1)}, u32[]{:S(2)}, u32[]{:S(2)}) %collective-permute-start.2) | collective-permute-done | bytes 139296 | tf_op jit(solution)/shard_map/ppermute | solution.py:533
  22.5 3.7 %collective-permute-start.5 = (f32[80,128]{1,0:T(8,128)S(1)}, f32[80,128]{1,0:T(8,128)S(1)}, u32[]{:S(2)}, u32[]{:S(2)}) collective-permute-start(f32[80,128]{1,0:T(8,128)S(1)} %get-tuple-element.35), channel_id=1, source_target_pairs={{0,3},{1,2},{2,1},{3,0},{4,7},{5,6},{6,5},{7,4},{8,11},{9,10},{10,... | collective-permute-start | bytes 122888 | tf_op jit(solution)/shard_map/ppermute | solution.py:533
  26.9 1.7 %copy-done = bf16[80,16,1024]{2,1,0:T(8,128)(2,1)S(1)} copy-done((bf16[80,16,1024]{2,1,0:T(8,128)(2,1)S(1)}, bf16[80,16,1024]{2,1,0:T(8,128)(2,1)}, u32[]{:S(2)}) %copy-start) | copy-done | bytes 2621464
  28.7 3.7 %observe.1 = (f32[4,88,128]{2,1,0:T(8,128)S(1)}, f32[4,88,128]{2,1,0:T(8,128)S(1)}) custom-call(bf16[1280,1024]{1,0:T(8,128)(2,1)S(1)} %bitcast.23, f32[16,1024]{1,0:T(8,128)S(1)} %copy-done.2, s32[4,512]{1,0:T(4,128)S(1)} %copy-done.4, s32[4,512]{1,0:T(4,128)S(1)} %copy-done.3), custom_call_target="tpu_custom_call" | custom-call | flops 4000000000 | bytes 10000000 | tf_op jit(solution)/shard_map/observe/pallas_call | solution.py:575
  33.9 1.7 %collective-permute-start.12 = (f32[4,88,128]{2,1,0:T(8,128)S(1)}, f32[4,88,128]{2,1,0:T(8,128)S(1)}, u32[]{:S(2)}, u32[]{:S(2)}) collective-permute-start(f32[4,88,128]{2,1,0:T(8,128)S(1)} %add.21), channel_id=1, source_target_pairs={{0,16},{8,24},{16,0},{24,8},{1,17},{9,25},{17,1},{25,9},{2,18},{10... | collective-permute-start | bytes 540680 | tf_op jit(solution)/shard_map/ppermute | solution.py:533
  35.6 9.0 %batch.3 = (bf16[16,96,256]{2,1,0:T(8,128)(2,1)S(1)}, f32[80,128]{1,0:T(8,128)S(1)}) custom-call(f32[272,128]{1,0:T(8,128)S(1)} %add.20.total_ref, f32[4,80,128]{2,1,0:T(8,128)S(1)} %pad_maximum_fusion.own_ref, f32[4,80,128]{2,1,0:T(8,128)S(1)} %collective-permute-done.6.peer_ref, s32[4,512]{1,0:T(4,128)S(1)} %copy-done.4, f32[4,512]{1,0:T(4,128)S(1)} %copy-done.5, ...), custom_call_target="tpu_custom_call" | custom-call | flops 10000000000 | bytes 10000000 | tf_op jit(solution)/shard_map/batch/pallas_call | solution.py:607
  44.6 3.7 %collective-permute-start.9 = (f32[80,128]{1,0:T(8,128)S(1)}, f32[80,128]{1,0:T(8,128)S(1)}, u32[]{:S(2)}, u32[]{:S(2)}) collective-permute-start(f32[80,128]{1,0:T(8,128)S(1)} %get-tuple-element.23), channel_id=1, source_target_pairs={{0,3},{1,2},{2,1},{3,0},{4,7},{5,6},{6,5},{7,4},{8,11},{9,10},{10,... | collective-permute-start | bytes 122888 | tf_op jit(solution)/shard_map/ppermute | solution.py:533
  49.1 1.6 %collective-permute-start.13 = (f32[4,88,128]{2,1,0:T(8,128)S(1)}, f32[4,88,128]{2,1,0:T(8,128)S(1)}, u32[]{:S(2)}, u32[]{:S(2)}) collective-permute-start(f32[4,88,128]{2,1,0:T(8,128)S(1)} %add.22), channel_id=1, source_target_pairs={{0,4},{4,0},{1,5},{5,1},{2,6},{6,2},{3,7},{7,3},{8,12},{12,8},{9,1... | collective-permute-start | bytes 540680 | tf_op jit(solution)/shard_map/ppermute | solution.py:533
  50.9 2.3 %collective-permute-done.8 = f32[80,128]{1,0:T(8,128)S(1)} collective-permute-done((f32[80,128]{1,0:T(8,128)S(1)}, f32[80,128]{1,0:T(8,128)S(1)}, u32[]{:S(2)}, u32[]{:S(2)}) %collective-permute-start.8) | collective-permute-done | bytes 40992 | tf_op jit(solution)/shard_map/ppermute | solution.py:533
  53.3 1.4 %copy.11 = bf16[80,16,1024]{2,0,1:T(8,128)(2,1)S(1)} copy(bf16[80,16,1024]{2,1,0:T(8,128)(2,1)S(1)} %copy-done.1) | data formatting | bytes 5242880 | tf_op jit(solution)/shard_map/optimization_barrier | solution.py:545
  54.8 10.0 %batch.4 = (bf16[16,96,512]{2,1,0:T(8,128)(2,1)S(1)}, f32[80,128]{1,0:T(8,128)S(1)}) custom-call(f32[272,128]{1,0:T(8,128)S(1)} %add.20.total_ref, f32[4,80,128]{2,1,0:T(8,128)S(1)} %pad_maximum_fusion.1.own_ref, f32[4,80,128]{2,1,0:T(8,128)S(1)} %collective-permute-done.10.peer_ref, bf16[16,96,256]{2,1,0:T(8,128)(2,1)S(1)} %get-tuple-element.26.refs_0_, ...), custom_call_target="tpu_custom_call" | custom-call | flops 10000000000 | bytes 10000000 | tf_op jit(solution)/shard_map/batch/pallas_call | solution.py:607
  64.8 3.5 %collective-permute-start.16 = (f32[80,128]{1,0:T(8,128)S(1)}, f32[80,128]{1,0:T(8,128)S(1)}, u32[]{:S(2)}, u32[]{:S(2)}) collective-permute-start(f32[80,128]{1,0:T(8,128)S(1)} %get-tuple-element.28), channel_id=1, source_target_pairs={{0,3},{1,2},{2,1},{3,0},{4,7},{5,6},{6,5},{7,4},{8,11},{9,10},{10,... | collective-permute-start | bytes 122888 | tf_op jit(solution)/shard_map/ppermute | solution.py:533
  69.2 1.5 %collective-permute-done.16 = f32[80,128]{1,0:T(8,128)S(1)} collective-permute-done((f32[80,128]{1,0:T(8,128)S(1)}, f32[80,128]{1,0:T(8,128)S(1)}, u32[]{:S(2)}, u32[]{:S(2)}) %collective-permute-start.16) | collective-permute-done | bytes 40992 | tf_op jit(solution)/shard_map/ppermute | solution.py:533
  70.8 2.5 %collective-permute-done.15 = f32[80,128]{1,0:T(8,128)S(1)} collective-permute-done((f32[80,128]{1,0:T(8,128)S(1)}, f32[80,128]{1,0:T(8,128)S(1)}, u32[]{:S(2)}, u32[]{:S(2)}) %collective-permute-start.15) | collective-permute-done | bytes 40992 | tf_op jit(solution)/shard_map/ppermute | solution.py:533
  73.3 1.4 %collective-permute-done.17.peer_ref = f32[4,80,128]{2,1,0:T(8,128)S(1)} collective-permute-done((f32[4,80,128]{2,1,0:T(8,128)S(1)}, f32[4,80,128]{2,1,0:T(8,128)S(1)}, u32[]{:S(2)}, u32[]{:S(2)}) %collective-permute-start.17) | collective-permute-done | bytes 163872 | tf_op jit(solution)/shard_map/ppermute | solution.py:533
  74.7 10.0 %batch.5 = (bf16[16,96,512]{2,1,0:T(8,128)(2,1)S(1)}, f32[80,128]{1,0:T(8,128)S(1)}) custom-call(f32[272,128]{1,0:T(8,128)S(1)} %add.20.total_ref, f32[4,80,128]{2,1,0:T(8,128)S(1)} %pad_maximum_fusion.2.own_ref, f32[4,80,128]{2,1,0:T(8,128)S(1)} %collective-permute-done.17.peer_ref, bf16[16,96,512]{2,1,0:T(8,128)(2,1)S(1)} %get-tuple-element.29.refs_0_, ...), custom_call_target="tpu_custom_call" | custom-call | flops 10000000000 | bytes 10000000 | tf_op jit(solution)/shard_map/batch/pallas_call | solution.py:607
  84.7 1.6 %collective-permute-start.20 = (f32[80,128]{1,0:T(8,128)S(1)}, f32[80,128]{1,0:T(8,128)S(1)}, u32[]{:S(2)}, u32[]{:S(2)}) collective-permute-start(f32[80,128]{1,0:T(8,128)S(1)} %get-tuple-element.30), channel_id=1, source_target_pairs={{0,3},{1,2},{2,1},{3,0},{4,7},{5,6},{6,5},{7,4},{8,11},{9,10},{10,... | collective-permute-start | bytes 122888 | tf_op jit(solution)/shard_map/ppermute | solution.py:533
  86.9 2.3 %collective-permute-start.18 = (f32[80,128]{1,0:T(8,128)S(1)}, f32[80,128]{1,0:T(8,128)S(1)}, u32[]{:S(2)}, u32[]{:S(2)}) collective-permute-start(f32[80,128]{1,0:T(8,128)S(1)} %get-tuple-element.30), channel_id=1, source_target_pairs={{0,1},{1,0},{2,3},{3,2},{4,5},{5,4},{6,7},{7,6},{8,9},{9,8},{10,11... | collective-permute-start | bytes 122888 | tf_op jit(solution)/shard_map/ppermute | solution.py:533
  89.2 1.8 %collective-permute-done.20 = f32[80,128]{1,0:T(8,128)S(1)} collective-permute-done((f32[80,128]{1,0:T(8,128)S(1)}, f32[80,128]{1,0:T(8,128)S(1)}, u32[]{:S(2)}, u32[]{:S(2)}) %collective-permute-start.20) | collective-permute-done | bytes 40992 | tf_op jit(solution)/shard_map/ppermute | solution.py:533
  93.4 10.0 %last.1 = (f32[16,1024]{1,0:T(8,128)}, bf16[1280,1024]{1,0:T(8,128)(2,1)}) custom-call(f32[272,128]{1,0:T(8,128)S(1)} %add.20.total_ref, f32[4,80,128]{2,1,0:T(8,128)S(1)} %pad_maximum_fusion.3.own_ref, f32[4,80,128]{2,1,0:T(8,128)S(1)} %collective-permute-done.21.peer_ref, bf16[16,96,512]{2,1,0:T(8,128)(2,1)S(1)} %get-tuple-element.31.old_ref, ...), custom_call_target="tpu_custom_call" | custom-call | tf_op jit(solution)/shard_map/last/pallas_call | solution.py:621
  (52 shorter events, 10.0 us)
Async XLA Ops:
  0.6 26.3 %copy-start.4 = (s32[4,512]{1,0:T(4,128)S(1)}, s32[4,512]{1,0:T(4,128)}, u32[]{:S(2)}) copy-start(s32[4,512]{1,0:T(4,128)} %refs_2_.7) | copy-start | bytes 24580
  0.6 26.3 %copy-start.2 = (f32[16,1024]{1,0:T(8,128)S(1)}, f32[16,1024]{1,0:T(8,128)}, u32[]{:S(2)}) copy-start(f32[16,1024]{1,0:T(8,128)} %mean_ref.3) | copy-start | bytes 196612
  7.5 1.7 %collective-permute-start = (f32[272,128]{1,0:T(8,128)}, f32[272,128]{1,0:T(8,128)S(1)}, u32[]{:S(2)}, u32[]{:S(2)}) collective-permute-start(f32[272,128]{1,0:T(8,128)} %get-tuple-element.19), channel_id=1, source_target_pairs={{0,8},{8,0},{16,24},{24,16},{1,9},{9,1},{17,25},{25,17},{2,10},{10... | collective-permute-start | bytes 417800 | tf_op jit(solution)/shard_map/ppermute | solution.py:533
  10.2 6.9 %collective-permute-start.1 = (f32[272,128]{1,0:T(8,128)S(1)}, f32[272,128]{1,0:T(8,128)S(1)}, u32[]{:S(2)}, u32[]{:S(2)}) collective-permute-start(f32[272,128]{1,0:T(8,128)S(1)} %add.18), channel_id=1, source_target_pairs={{0,16},{8,24},{16,0},{24,8},{1,17},{9,25},{17,1},{25,9},{2,18},{10... | collective-permute-start | bytes 417800 | tf_op jit(solution)/shard_map/ppermute | solution.py:533
  17.1 5.3 %collective-permute-start.2 = (f32[272,128]{1,0:T(8,128)S(1)}, f32[272,128]{1,0:T(8,128)S(1)}, u32[]{:S(2)}, u32[]{:S(2)}) collective-permute-start(f32[272,128]{1,0:T(8,128)S(1)} %add.19), channel_id=1, source_target_pairs={{0,4},{4,0},{1,5},{5,1},{2,6},{6,2},{3,7},{7,3},{8,12},{12,8},{9,1... | collective-permute-start | bytes 417800 | tf_op jit(solution)/shard_map/ppermute | solution.py:533
  22.5 10.0 %collective-permute-start.5 = (f32[80,128]{1,0:T(8,128)S(1)}, f32[80,128]{1,0:T(8,128)S(1)}, u32[]{:S(2)}, u32[]{:S(2)}) collective-permute-start(f32[80,128]{1,0:T(8,128)S(1)} %get-tuple-element.35), channel_id=1, source_target_pairs={{0,3},{1,2},{2,1},{3,0},{4,7},{5,6},{6,5},{7,4},{8,11},{9,10},{10,... | collective-permute-start | bytes 122888 | tf_op jit(solution)/shard_map/ppermute | solution.py:533
  26.2 6.3 %collective-permute-start.4 = (f32[80,128]{1,0:T(8,128)S(1)}, f32[80,128]{1,0:T(8,128)S(1)}, u32[]{:S(2)}, u32[]{:S(2)}) collective-permute-start(f32[80,128]{1,0:T(8,128)S(1)} %get-tuple-element.35), channel_id=1, source_target_pairs={{0,2},{1,3},{2,0},{3,1},{4,6},{5,7},{6,4},{7,5},{8,10},{9,11},{10,... | collective-permute-start | bytes 122888 | tf_op jit(solution)/shard_map/ppermute | solution.py:533
  26.2 6.3 %collective-permute-start.3 = (f32[80,128]{1,0:T(8,128)S(1)}, f32[80,128]{1,0:T(8,128)S(1)}, u32[]{:S(2)}, u32[]{:S(2)}) collective-permute-start(f32[80,128]{1,0:T(8,128)S(1)} %get-tuple-element.35), channel_id=1, source_target_pairs={{0,1},{1,0},{2,3},{3,2},{4,5},{5,4},{6,7},{7,6},{8,9},{9,8},{10,11... | collective-permute-start | bytes 122888 | tf_op jit(solution)/shard_map/ppermute | solution.py:533
  32.4 1.5 %collective-permute-start.11 = (f32[4,88,128]{2,1,0:T(8,128)S(1)}, f32[4,88,128]{2,1,0:T(8,128)S(1)}, u32[]{:S(2)}, u32[]{:S(2)}) collective-permute-start(f32[4,88,128]{2,1,0:T(8,128)S(1)} %get-tuple-element.27), channel_id=1, source_target_pairs={{0,8},{8,0},{16,24},{24,16},{1,9},{9,1},{17,25},{25,17},{2,10},{10... | collective-permute-start | bytes 540680 | tf_op jit(solution)/shard_map/ppermute | solution.py:533
  32.5 3.0 %collective-permute-start.6 = (f32[4,80,128]{2,1,0:T(8,128)S(1)}, f32[4,80,128]{2,1,0:T(8,128)S(1)}, u32[]{:S(2)}, u32[]{:S(2)}) collective-permute-start(f32[4,80,128]{2,1,0:T(8,128)S(1)} %pad_maximum_fusion.own_ref), channel_id=1, source_target_pairs={{0,8},{8,0},{16,24},{24,16},{1,9},{9,1},{17,25},{25,17},{2,10},{10... | collective-permute-start | bytes 491528 | tf_op jit(solution)/shard_map/ppermute | solution.py:533
  33.9 15.1 %collective-permute-start.12 = (f32[4,88,128]{2,1,0:T(8,128)S(1)}, f32[4,88,128]{2,1,0:T(8,128)S(1)}, u32[]{:S(2)}, u32[]{:S(2)}) collective-permute-start(f32[4,88,128]{2,1,0:T(8,128)S(1)} %add.21), channel_id=1, source_target_pairs={{0,16},{8,24},{16,0},{24,8},{1,17},{9,25},{17,1},{25,9},{2,18},{10... | collective-permute-start | bytes 540680 | tf_op jit(solution)/shard_map/ppermute | solution.py:533
  44.6 6.3 %collective-permute-start.9 = (f32[80,128]{1,0:T(8,128)S(1)}, f32[80,128]{1,0:T(8,128)S(1)}, u32[]{:S(2)}, u32[]{:S(2)}) collective-permute-start(f32[80,128]{1,0:T(8,128)S(1)} %get-tuple-element.23), channel_id=1, source_target_pairs={{0,3},{1,2},{2,1},{3,0},{4,7},{5,6},{6,5},{7,4},{8,11},{9,10},{10,... | collective-permute-start | bytes 122888 | tf_op jit(solution)/shard_map/ppermute | solution.py:533
  48.3 4.9 %collective-permute-start.8 = (f32[80,128]{1,0:T(8,128)S(1)}, f32[80,128]{1,0:T(8,128)S(1)}, u32[]{:S(2)}, u32[]{:S(2)}) collective-permute-start(f32[80,128]{1,0:T(8,128)S(1)} %get-tuple-element.23), channel_id=1, source_target_pairs={{0,2},{1,3},{2,0},{3,1},{4,6},{5,7},{6,4},{7,5},{8,10},{9,11},{10,... | collective-permute-start | bytes 122888 | tf_op jit(solution)/shard_map/ppermute | solution.py:533
  48.3 4.9 %collective-permute-start.7 = (f32[80,128]{1,0:T(8,128)S(1)}, f32[80,128]{1,0:T(8,128)S(1)}, u32[]{:S(2)}, u32[]{:S(2)}) collective-permute-start(f32[80,128]{1,0:T(8,128)S(1)} %get-tuple-element.23), channel_id=1, source_target_pairs={{0,1},{1,0},{2,3},{3,2},{4,5},{5,4},{6,7},{7,6},{8,9},{9,8},{10,11... | collective-permute-start | bytes 122888 | tf_op jit(solution)/shard_map/ppermute | solution.py:533
  49.1 5.7 %collective-permute-start.13 = (f32[4,88,128]{2,1,0:T(8,128)S(1)}, f32[4,88,128]{2,1,0:T(8,128)S(1)}, u32[]{:S(2)}, u32[]{:S(2)}) collective-permute-start(f32[4,88,128]{2,1,0:T(8,128)S(1)} %add.22), channel_id=1, source_target_pairs={{0,4},{4,0},{1,5},{5,1},{2,6},{6,2},{3,7},{7,3},{8,12},{12,8},{9,1... | collective-permute-start | bytes 540680 | tf_op jit(solution)/shard_map/ppermute | solution.py:533
  53.2 1.6 %collective-permute-start.10 = (f32[4,80,128]{2,1,0:T(8,128)S(1)}, f32[4,80,128]{2,1,0:T(8,128)S(1)}, u32[]{:S(2)}, u32[]{:S(2)}) collective-permute-start(f32[4,80,128]{2,1,0:T(8,128)S(1)} %pad_maximum_fusion.1.own_ref), channel_id=1, source_target_pairs={{0,8},{8,0},{16,24},{24,16},{1,9},{9,1},{17,25},{25,17},{2,10},{10... | collective-permute-start | bytes 491528 | tf_op jit(solution)/shard_map/ppermute | solution.py:533
  64.8 6.0 %collective-permute-start.16 = (f32[80,128]{1,0:T(8,128)S(1)}, f32[80,128]{1,0:T(8,128)S(1)}, u32[]{:S(2)}, u32[]{:S(2)}) collective-permute-start(f32[80,128]{1,0:T(8,128)S(1)} %get-tuple-element.28), channel_id=1, source_target_pairs={{0,3},{1,2},{2,1},{3,0},{4,7},{5,6},{6,5},{7,4},{8,11},{9,10},{10,... | collective-permute-start | bytes 122888 | tf_op jit(solution)/shard_map/ppermute | solution.py:533
  68.3 4.9 %collective-permute-start.15 = (f32[80,128]{1,0:T(8,128)S(1)}, f32[80,128]{1,0:T(8,128)S(1)}, u32[]{:S(2)}, u32[]{:S(2)}) collective-permute-start(f32[80,128]{1,0:T(8,128)S(1)} %get-tuple-element.28), channel_id=1, source_target_pairs={{0,2},{1,3},{2,0},{3,1},{4,6},{5,7},{6,4},{7,5},{8,10},{9,11},{10,... | collective-permute-start | bytes 122888 | tf_op jit(solution)/shard_map/ppermute | solution.py:533
  68.3 4.9 %collective-permute-start.14 = (f32[80,128]{1,0:T(8,128)S(1)}, f32[80,128]{1,0:T(8,128)S(1)}, u32[]{:S(2)}, u32[]{:S(2)}) collective-permute-start(f32[80,128]{1,0:T(8,128)S(1)} %get-tuple-element.28), channel_id=1, source_target_pairs={{0,1},{1,0},{2,3},{3,2},{4,5},{5,4},{6,7},{7,6},{8,9},{9,8},{10,11... | collective-permute-start | bytes 122888 | tf_op jit(solution)/shard_map/ppermute | solution.py:533
  73.2 1.5 %collective-permute-start.17 = (f32[4,80,128]{2,1,0:T(8,128)S(1)}, f32[4,80,128]{2,1,0:T(8,128)S(1)}, u32[]{:S(2)}, u32[]{:S(2)}) collective-permute-start(f32[4,80,128]{2,1,0:T(8,128)S(1)} %pad_maximum_fusion.2.own_ref), channel_id=1, source_target_pairs={{0,8},{8,0},{16,24},{24,16},{1,9},{9,1},{17,25},{25,17},{2,10},{10... | collective-permute-start | bytes 491528 | tf_op jit(solution)/shard_map/ppermute | solution.py:533
  84.7 6.3 %collective-permute-start.20 = (f32[80,128]{1,0:T(8,128)S(1)}, f32[80,128]{1,0:T(8,128)S(1)}, u32[]{:S(2)}, u32[]{:S(2)}) collective-permute-start(f32[80,128]{1,0:T(8,128)S(1)} %get-tuple-element.30), channel_id=1, source_target_pairs={{0,3},{1,2},{2,1},{3,0},{4,7},{5,6},{6,5},{7,4},{8,11},{9,10},{10,... | collective-permute-start | bytes 122888 | tf_op jit(solution)/shard_map/ppermute | solution.py:533
  86.4 5.6 %collective-permute-start.19 = (f32[80,128]{1,0:T(8,128)S(1)}, f32[80,128]{1,0:T(8,128)S(1)}, u32[]{:S(2)}, u32[]{:S(2)}) collective-permute-start(f32[80,128]{1,0:T(8,128)S(1)} %get-tuple-element.30), channel_id=1, source_target_pairs={{0,2},{1,3},{2,0},{3,1},{4,6},{5,7},{6,4},{7,5},{8,10},{9,11},{10,... | collective-permute-start | bytes 122888 | tf_op jit(solution)/shard_map/ppermute | solution.py:533
  86.9 5.1 %collective-permute-start.18 = (f32[80,128]{1,0:T(8,128)S(1)}, f32[80,128]{1,0:T(8,128)S(1)}, u32[]{:S(2)}, u32[]{:S(2)}) collective-permute-start(f32[80,128]{1,0:T(8,128)S(1)} %get-tuple-element.30), channel_id=1, source_target_pairs={{0,1},{1,0},{2,3},{3,2},{4,5},{5,4},{6,7},{7,6},{8,9},{9,8},{10,11... | collective-permute-start | bytes 122888 | tf_op jit(solution)/shard_map/ppermute | solution.py:533
  92.0 1.5 %collective-permute-start.21 = (f32[4,80,128]{2,1,0:T(8,128)S(1)}, f32[4,80,128]{2,1,0:T(8,128)S(1)}, u32[]{:S(2)}, u32[]{:S(2)}) collective-permute-start(f32[4,80,128]{2,1,0:T(8,128)S(1)} %pad_maximum_fusion.3.own_ref), channel_id=1, source_target_pairs={{0,8},{8,0},{16,24},{24,16},{1,9},{9,1},{17,25},{25,17},{2,10},{10... | collective-permute-start | bytes 491528 | tf_op jit(solution)/shard_map/ppermute | solution.py:533
  (5 other events, 72.0 us)
